TPU v7x, 256 devices: a whole 4x4x8 slice. The times are simulated.
256 devices in a mesh: rad: 8 (over y, x_hi), az: 32 (over z, x_lo, core).
Axes of the slice: x: 4 (x_hi: 2, x_lo: 2; x = x_hi * 2 + x_lo), y: 4, z: 8, core: 2. Of those that a mesh axis runs over, the one named last changes fastest.
Arguments:
- state: float32 [8, 8, 128, 4096], P(None, None, 'rad', 'az'), may hold values from -1.6 to 2, as said below
- shift: int32 [128], P('rad'), may hold values from 0 to 4095, as said below
Outputs:
- advanced: float32 [8, 8, 128, 4096], P(None, None, 'rad', 'az')
Inputs may be any that keep to these rules, and one draw needn't show every extreme that they name: `state`: components: density (0) in 0.5 to 2, momentum (1 to 3) within 1.2 in magnitude, face fields (4 to 6) within 1.6 in magnitude, tracer (7) in 0 to 1. In each aligned block of the 16 rows of one device, at most 2 rows have the same value of shift // 128, and exactly 2 rows share one such value.
All inputs are finite; a program needn't handle non-finite values.
Results may differ from a plain program's by a relative error of at most 0.0003.
Values sent between devices are 32-bit elements; how exact they have to be, the bound alone decides.
A program may use at most 128 MiB of HBM per device.

v0:
```python
import jax
import jax.numpy as jnp
from jax import lax
from jax.sharding import PartitionSpec as P

sound_sq = 1.0
time_step = 0.05
axis_of = (1, 2, 0)


def passed_along(value, axis, steps):
    count = lax.axis_size(axis)
    pairs = [(source, (source + steps) % count) for source in range(count)]
    return lax.ppermute(value, axis, pairs)


def with_halo(block, sides, width, periodic):
    for axis, dim in sides:
        count = lax.axis_size(axis)
        forward = [(i, i + 1) for i in range(count - 1)]
        if periodic:
            forward.append((count - 1, 0))
        backward = [(target, source) for source, target in forward]
        low = lax.ppermute(
            lax.slice_in_dim(block, block.shape[dim] - width, None, axis=dim), axis, forward
        )
        high = lax.ppermute(lax.slice_in_dim(block, 0, width, axis=dim), axis, backward)
        block = jnp.concatenate([low, block, high], axis=dim)
    return block


def next_cell(values, direc):
    return jnp.roll(values, -1, axis_of[direc])


def prev_cell(values, direc):
    return jnp.roll(values, 1, axis_of[direc])


def physical(density, moment, center, tracer, normal, direc):
    velocity = [moment[k] / density for k in range(3)]
    fields = [normal if k == direc else center[k] for k in range(3)]
    square = fields[0] * fields[0] + fields[1] * fields[1] + fields[2] * fields[2]
    normal_speed = velocity[direc]
    mass_flux = moment[direc]
    moment_flux = [moment[k] * normal_speed - fields[k] * normal for k in range(3)]
    moment_flux[direc] = moment_flux[direc] + sound_sq * density + 0.5 * square
    induce = [normal_speed * fields[k] - velocity[k] * normal for k in range(3)]
    signal = jnp.abs(normal_speed) + jnp.sqrt(sound_sq + square / density)
    return (mass_flux, moment_flux, induce, tracer * normal_speed, signal)


def rusanov(density, moment, center, tracer, faces, direc):
    normal = faces[direc]
    left_density = prev_cell(density, direc)
    left_moment = [prev_cell(moment[k], direc) for k in range(3)]
    left_center = [prev_cell(center[k], direc) for k in range(3)]
    left_tracer = prev_cell(tracer, direc)
    left = physical(left_density, left_moment, left_center, left_tracer, normal, direc)
    right = physical(density, moment, center, tracer, normal, direc)
    signal = jnp.maximum(left[4], right[4])
    mass_flux = 0.5 * (left[0] + right[0]) - 0.5 * signal * (density - left_density)
    moment_flux = [
        0.5 * (left[1][k] + right[1][k]) - 0.5 * signal * (moment[k] - left_moment[k])
        for k in range(3)
    ]
    induce = [
        0.5 * (left[2][k] + right[2][k]) - 0.5 * signal * (center[k] - left_center[k])
        for k in range(3)
    ]
    tracer_flux = 0.5 * (left[3] + right[3]) - 0.5 * signal * (tracer - left_tracer)
    return (mass_flux, moment_flux, induce, tracer_flux)


def divergence(terms):
    total = next_cell(terms[0], 0) - terms[0]
    for direc in (1, 2):
        total = total + (next_cell(terms[direc], direc) - terms[direc])
    return total


def advance(block):
    density = block[0]
    moment = [block[1], block[2], block[3]]
    faces = [block[4], block[5], block[6]]
    tracer = block[7]
    center = [0.5 * (faces[k] + next_cell(faces[k], k)) for k in range(3)]
    fluxes = [rusanov(density, moment, center, tracer, faces, direc) for direc in range(3)]
    new_density = density - time_step * divergence([fluxes[d][0] for d in range(3)])
    new_moment = [
        moment[k] - time_step * divergence([fluxes[d][1][k] for d in range(3)]) for k in range(3)
    ]
    new_tracer = tracer - time_step * divergence([fluxes[d][3] for d in range(3)])
    induce = [fluxes[d][2] for d in range(3)]
    edge_two = 0.25 * (
        induce[1][0] + prev_cell(induce[1][0], 0) - (induce[0][1] + prev_cell(induce[0][1], 1))
    )
    edge_zero = 0.25 * (
        induce[2][1] + prev_cell(induce[2][1], 1) - (induce[1][2] + prev_cell(induce[1][2], 2))
    )
    edge_one = 0.25 * (
        induce[0][2] + prev_cell(induce[0][2], 2) - (induce[2][0] + prev_cell(induce[2][0], 0))
    )
    face_zero = faces[0] - time_step * (
        next_cell(edge_two, 1) - edge_two - (next_cell(edge_one, 2) - edge_one)
    )
    face_one = faces[1] - time_step * (
        next_cell(edge_zero, 2) - edge_zero - (next_cell(edge_two, 0) - edge_two)
    )
    face_two = faces[2] - time_step * (
        next_cell(edge_one, 0) - edge_one - (next_cell(edge_zero, 1) - edge_zero)
    )
    result = jnp.stack(
        [new_density] + new_moment + [face_zero, face_one, face_two, new_tracer], axis=0
    )
    return result[:, :, 2:-2, 2:-2]


def outflow(padded, place, last_place):
    inner = padded[:, :, 2:-2]
    lower = jnp.where(
        place == 0, jnp.broadcast_to(inner[:, :, :1], padded[:, :, :2].shape), padded[:, :, :2]
    )
    upper = jnp.where(
        place == last_place,
        jnp.broadcast_to(inner[:, :, -1:], padded[:, :, -2:].shape),
        padded[:, :, -2:],
    )
    return jnp.concatenate([lower, inner, upper], axis=2)


def rotate_local(values, amount):
    row_width = values.shape[-1]
    last_axis = values.ndim - 1
    for bit_level in range((row_width - 1).bit_length()):
        rolled = jnp.roll(values, 1 << bit_level, axis=last_axis)
        chosen = amount // (1 << bit_level) % 2 == 1
        values = jnp.where(chosen[:, None], rolled, values)
    return values


def per_device(state, shift):
    row_count = state.shape[2]
    col_count = state.shape[3]
    column = lax.broadcasted_iota(jnp.int32, (row_count, col_count), 1)
    residual = shift % col_count
    coarse = shift // col_count
    rolled = rotate_local(state, residual)
    carried = passed_along(rolled, "az", 1)
    remapped = jnp.where((column >= residual[:, None])[None, None], rolled, carried)
    for bit_level in range((lax.axis_size("az") - 1).bit_length()):
        arrived = passed_along(remapped, "az", 1 << bit_level)
        chosen = coarse // (1 << bit_level) % 2 == 1
        remapped = jnp.where(chosen[None, None, :, None], arrived, remapped)
    place = lax.axis_index("rad")
    last_place = lax.axis_size("rad") - 1
    radial = with_halo(remapped, (("rad", 2),), 2, False)
    radial = outflow(radial, place, last_place)
    extended = with_halo(radial, (("az", 3),), 2, True)
    return advance(extended)


def solution(mesh):
    placed = (P(None, None, "rad", "az"), P("rad"))
    return jax.shard_map(
        per_device,
        mesh=mesh,
        in_specs=placed,
        out_specs=P(None, None, "rad", "az"),
        check_vma=False,
    )
```

profile of v0, /device:TPU:109, one launch (start us, length us, event | category | flops | bytes accessed | tf_op | source)
XLA Modules:
  0.0 245.5 jit_solution(7854418708098325883)
XLA Ops:
  0.8 1.2 slice.610
  5.3 1.6 collective-permute-start
  6.9 6.1 %collective-permute-done = f32[8,8,16,128]{3,1,0,2:T(8,128)S(1)} collective-permute-done((f32[8,8,16,128]{3,1,0,2:T(8,128)S(1)}, f32[8,8,16,128]{3,1,0,2:T(8,128)S(1)}, u32[]{:S(2)}, u32[]{:S(2)}) %collective-permute-start) | collective-permute-done | bytes 524320 | tf_op jit(solution)/shard_map/ppermute | solution.py:14
  13.0 2.6 %collective-permute-start.1 = (f32[8,8,16,128]{3,1,0,2:T(8,128)S(1)}, f32[8,8,16,128]{3,1,0,2:T(8,128)S(1)}, u32[]{:S(2)}, u32[]{:S(2)}) collective-permute-start(f32[8,8,16,128]{3,1,0,2:T(8,128)S(1)} %broadcast_select_fusion.5), channel_id=1, source_target_pairs={{0,1},{1,2},{2,3},{3,4},{4,5},{5,6},{6,7},{7,8},{8,9},{9,10},{10,1... | collective-permute-start | bytes 1572872 | tf_op jit(solution)/shard_map/ppermute | solution.py:14
  15.6 6.1 %collective-permute-done.1 = f32[8,8,16,128]{3,1,0,2:T(8,128)S(1)} collective-permute-done((f32[8,8,16,128]{3,1,0,2:T(8,128)S(1)}, f32[8,8,16,128]{3,1,0,2:T(8,128)S(1)}, u32[]{:S(2)}, u32[]{:S(2)}) %collective-permute-start.1) | collective-permute-done | bytes 524320 | tf_op jit(solution)/shard_map/ppermute | solution.py:14
  21.8 5.3 %collective-permute-start.2 = (f32[8,8,16,128]{3,1,0,2:T(8,128)S(1)}, f32[8,8,16,128]{3,1,0,2:T(8,128)S(1)}, u32[]{:S(2)}, u32[]{:S(2)}) collective-permute-start(f32[8,8,16,128]{3,1,0,2:T(8,128)S(1)} %broadcast_select_fusion), channel_id=1, source_target_pairs={{0,2},{1,3},{2,4},{3,5},{4,6},{5,7},{6,8},{7,9},{8,10},{9,11},{10,... | collective-permute-start | bytes 1572872 | tf_op jit(solution)/shard_map/ppermute | solution.py:14
  27.1 10.2 %collective-permute-done.2 = f32[8,8,16,128]{3,1,0,2:T(8,128)S(1)} collective-permute-done((f32[8,8,16,128]{3,1,0,2:T(8,128)S(1)}, f32[8,8,16,128]{3,1,0,2:T(8,128)S(1)}, u32[]{:S(2)}, u32[]{:S(2)}) %collective-permute-start.2) | collective-permute-done | bytes 524320 | tf_op jit(solution)/shard_map/ppermute | solution.py:14
  37.5 13.6 %collective-permute-done.3 = f32[8,8,16,128]{3,1,0,2:T(8,128)S(1)} collective-permute-done((f32[8,8,16,128]{3,1,0,2:T(8,128)S(1)}, f32[8,8,16,128]{3,1,0,2:T(8,128)S(1)}, u32[]{:S(2)}, u32[]{:S(2)}) %collective-permute-start.3) | collective-permute-done | bytes 524320 | tf_op jit(solution)/shard_map/ppermute | solution.py:14
  51.4 36.4 %collective-permute-done.4 = f32[8,8,16,128]{3,1,0,2:T(8,128)S(1)} collective-permute-done((f32[8,8,16,128]{3,1,0,2:T(8,128)S(1)}, f32[8,8,16,128]{3,1,0,2:T(8,128)S(1)}, u32[]{:S(2)}, u32[]{:S(2)}) %collective-permute-start.4) | collective-permute-done | bytes 524320 | tf_op jit(solution)/shard_map/ppermute | solution.py:14
  88.0 21.0 %collective-permute-done.5 = f32[8,8,16,128]{3,1,0,2:T(8,128)S(1)} collective-permute-done((f32[8,8,16,128]{3,1,0,2:T(8,128)S(1)}, f32[8,8,16,128]{3,1,0,2:T(8,128)S(1)}, u32[]{:S(2)}, u32[]{:S(2)}) %collective-permute-start.5) | collective-permute-done | bytes 524320 | tf_op jit(solution)/shard_map/ppermute | solution.py:14
  109.1 1.9 collective-permute-start.6
  111.1 4.9 %collective-permute-start.7 = (f32[8,8,2,128]{3,1,0,2:T(8,128)S(1)}, f32[8,8,2,128]{3,1,0,2:T(8,128)S(1)}, u32[]{:S(2)}, u32[]{:S(2)}) collective-permute-start(f32[8,8,2,128]{3,1,0,2:T(8,128)S(1)} %get-tuple-element.84), channel_id=1, source_target_pairs={{32,0},{64,32},{96,64},{128,96},{160,128},{192,160},{224,192},{33,... | collective-permute-start | bytes 196616 | tf_op jit(solution)/shard_map/ppermute | solution.py:27
  116.0 2.5 %collective-permute-done.7 = f32[8,8,2,128]{3,1,0,2:T(8,128)S(1)} collective-permute-done((f32[8,8,2,128]{3,1,0,2:T(8,128)S(1)}, f32[8,8,2,128]{3,1,0,2:T(8,128)S(1)}, u32[]{:S(2)}, u32[]{:S(2)}) %collective-permute-start.7) | collective-permute-done | bytes 65568 | tf_op jit(solution)/shard_map/ppermute | solution.py:27
  119.4 22.5 %collective-permute-start.8 = (f32[8,8,20,2]{2,1,3,0:T(8,128)S(1)}, f32[8,8,20,2]{2,1,3,0:T(8,128)S(1)}, u32[]{:S(2)}, u32[]{:S(2)}) collective-permute-start(f32[8,8,20,2]{2,1,3,0:T(8,128)S(1)} %copy.1015), channel_id=1, source_target_pairs={{0,1},{1,2},{2,3},{3,4},{4,5},{5,6},{6,7},{7,8},{8,9},{9,10},{10,1... | collective-permute-start | bytes 30728 | tf_op jit(solution)/shard_map/ppermute | solution.py:24
  143.9 2.4 collective-permute-done.9
  149.2 0.8 slice_bitcast_fusion.91
  153.4 1.0 fusion.247
  154.4 1.1 multiply_subtract_fusion
  155.4 0.9 multiply_subtract_fusion.7
  158.1 0.8 slice_bitcast_fusion.75
  159.1 0.8 slice_bitcast_fusion.83
  159.8 1.0 multiply_subtract_fusion.1
  160.9 0.9 multiply_subtract_fusion.3
  163.2 0.9 fusion.133
  169.1 0.8 slice_bitcast_fusion.64
  169.8 0.9 multiply_subtract_fusion.2
  172.3 0.8 multiply_subtract_fusion.4
  176.9 0.9 multiply_subtract_fusion.6
  179.9 0.8 slice_bitcast_fusion.5
  180.7 1.0 copy.1089
  181.7 1.6 slice.695
  183.3 1.7 slice_bitcast_fusion.7
  185.0 1.2 multiply_subtract_fusion.9
  192.7 0.8 slice_bitcast_fusion.11
  196.4 0.9 multiply_subtract_fusion.10
  198.0 0.8 slice_bitcast_fusion.13
  202.9 1.6 copy.1035
  204.5 1.6 copy.1056
  206.7 0.8 slice_bitcast_fusion.9
  208.8 1.0 copy.1077
  211.1 1.0 copy.1105
  212.1 0.8 slice_bitcast_fusion.2
  214.2 0.8 slice_bitcast_fusion.1
  215.0 1.6 slice_bitcast_fusion.14
  216.6 1.3 slice_bitcast_fusion.47
  219.5 0.8 copy.1084
  220.3 0.8 copy.1090
  221.2 0.8 copy.1076
  222.1 0.8 copy.1055
  223.0 0.8 copy.1032
  223.8 0.8 copy.1042
  224.6 0.8 copy.1038
  225.3 0.8 copy.1027
  226.1 0.8 copy.1034
  227.6 0.8 copy.1057
  228.5 0.8 copy.1067
  229.3 0.8 copy.1078
  230.1 0.8 copy.1106
  231.0 0.8 copy.1121
  231.9 0.8 copy.1126
  232.6 0.8 copy.1128
  233.5 3.3 %fusion.8 = (f32[8,8,20,132]{3,1,0,2:T(8,128)S(1)}, f32[1,8,20,132]{3,1,2,0:T(8,128)S(1)}, f32[1,8,20,132]{3,1,2,0:T(8,128)S(1)}, f32[1,8,20,132]{3,1,2,0:T(8,12...) fusion(f32[1,8,1,132]{3,1,2,0:T(8,128)} %slice_bitcast_fusion.5, ...), kind=kLoop, calls=%fused_computation.31 | loop fusion | flops 2238719 | bytes 4405760
  241.2 0.8 fusion.38
  244.4 1.1 copy.1141
  (482 shorter events, 57.3 us)
Async XLA Ops:
  5.3 7.7 %collective-permute-start = (f32[8,8,16,128]{3,1,0,2:T(8,128)S(1)}, f32[8,8,16,128]{3,1,0,2:T(8,128)S(1)}, u32[]{:S(2)}, u32[]{:S(2)}) collective-permute-start(f32[8,8,16,128]{3,1,0,2:T(8,128)S(1)} %maximum_select_fusion.6), channel_id=1, source_target_pairs={{0,1},{1,2},{2,3},{3,4},{4,5},{5,6},{6,7},{7,8},{8,9},{9,10},{10,1... | collective-permute-start | bytes 1572872 | tf_op jit(solution)/shard_map/ppermute | solution.py:14
  13.0 8.7 %collective-permute-start.1 = (f32[8,8,16,128]{3,1,0,2:T(8,128)S(1)}, f32[8,8,16,128]{3,1,0,2:T(8,128)S(1)}, u32[]{:S(2)}, u32[]{:S(2)}) collective-permute-start(f32[8,8,16,128]{3,1,0,2:T(8,128)S(1)} %broadcast_select_fusion.5), channel_id=1, source_target_pairs={{0,1},{1,2},{2,3},{3,4},{4,5},{5,6},{6,7},{7,8},{8,9},{9,10},{10,1... | collective-permute-start | bytes 1572872 | tf_op jit(solution)/shard_map/ppermute | solution.py:14
  21.8 15.5 %collective-permute-start.2 = (f32[8,8,16,128]{3,1,0,2:T(8,128)S(1)}, f32[8,8,16,128]{3,1,0,2:T(8,128)S(1)}, u32[]{:S(2)}, u32[]{:S(2)}) collective-permute-start(f32[8,8,16,128]{3,1,0,2:T(8,128)S(1)} %broadcast_select_fusion), channel_id=1, source_target_pairs={{0,2},{1,3},{2,4},{3,5},{4,6},{5,7},{6,8},{7,9},{8,10},{9,11},{10,... | collective-permute-start | bytes 1572872 | tf_op jit(solution)/shard_map/ppermute | solution.py:14
  37.4 13.7 %collective-permute-start.3 = (f32[8,8,16,128]{3,1,0,2:T(8,128)S(1)}, f32[8,8,16,128]{3,1,0,2:T(8,128)S(1)}, u32[]{:S(2)}, u32[]{:S(2)}) collective-permute-start(f32[8,8,16,128]{3,1,0,2:T(8,128)S(1)} %broadcast_select_fusion.1), channel_id=1, source_target_pairs={{0,4},{1,5},{2,6},{3,7},{4,8},{5,9},{6,10},{7,11},{8,12},{9,13},{1... | collective-permute-start | bytes 1572872 | tf_op jit(solution)/shard_map/ppermute | solution.py:14
  51.3 36.5 %collective-permute-start.4 = (f32[8,8,16,128]{3,1,0,2:T(8,128)S(1)}, f32[8,8,16,128]{3,1,0,2:T(8,128)S(1)}, u32[]{:S(2)}, u32[]{:S(2)}) collective-permute-start(f32[8,8,16,128]{3,1,0,2:T(8,128)S(1)} %broadcast_select_fusion.2), channel_id=1, source_target_pairs={{0,8},{1,9},{2,10},{3,11},{4,12},{5,13},{6,14},{7,15},{8,16},{9,17... | collective-permute-start | bytes 1572872 | tf_op jit(solution)/shard_map/ppermute | solution.py:14
  87.9 21.1 %collective-permute-start.5 = (f32[8,8,16,128]{3,1,0,2:T(8,128)S(1)}, f32[8,8,16,128]{3,1,0,2:T(8,128)S(1)}, u32[]{:S(2)}, u32[]{:S(2)}) collective-permute-start(f32[8,8,16,128]{3,1,0,2:T(8,128)S(1)} %broadcast_select_fusion.3), channel_id=1, source_target_pairs={{0,16},{1,17},{2,18},{3,19},{4,20},{5,21},{6,22},{7,23},{8,24},{9,... | collective-permute-start | bytes 1572872 | tf_op jit(solution)/shard_map/ppermute | solution.py:14
  109.1 6.8 %collective-permute-start.6 = (f32[8,8,2,128]{3,1,0,2:T(8,128)S(1)}, f32[8,8,2,128]{3,1,0,2:T(8,128)S(1)}, u32[]{:S(2)}, u32[]{:S(2)}) collective-permute-start(f32[8,8,2,128]{3,1,0,2:T(8,128)S(1)} %get-tuple-element.83), channel_id=1, source_target_pairs={{0,32},{32,64},{64,96},{96,128},{128,160},{160,192},{192,224},{1,3... | collective-permute-start | bytes 196616 | tf_op jit(solution)/shard_map/ppermute | solution.py:24
  111.1 7.4 %collective-permute-start.7 = (f32[8,8,2,128]{3,1,0,2:T(8,128)S(1)}, f32[8,8,2,128]{3,1,0,2:T(8,128)S(1)}, u32[]{:S(2)}, u32[]{:S(2)}) collective-permute-start(f32[8,8,2,128]{3,1,0,2:T(8,128)S(1)} %get-tuple-element.84), channel_id=1, source_target_pairs={{32,0},{64,32},{96,64},{128,96},{160,128},{192,160},{224,192},{33,... | collective-permute-start | bytes 196616 | tf_op jit(solution)/shard_map/ppermute | solution.py:27
  116.0 31.1 %copy-start.41 = (f32[8,8,2,128]{3,1,0,2:T(8,128)}, f32[8,8,2,128]{3,1,0,2:T(8,128)S(1)}, u32[]{:S(2)}) copy-start(f32[8,8,2,128]{3,1,0,2:T(8,128)S(1)} %broadcast_select_fusion.7) | copy-start | bytes 196612
  118.5 28.6 %copy-start.43 = (f32[8,8,2,128]{3,1,0,2:T(8,128)}, f32[8,8,2,128]{3,1,0,2:T(8,128)S(1)}, u32[]{:S(2)}) copy-start(f32[8,8,2,128]{3,1,0,2:T(8,128)S(1)} %broadcast_select_fusion.6) | copy-start | bytes 196612
  119.4 23.8 %collective-permute-start.8 = (f32[8,8,20,2]{2,1,3,0:T(8,128)S(1)}, f32[8,8,20,2]{2,1,3,0:T(8,128)S(1)}, u32[]{:S(2)}, u32[]{:S(2)}) collective-permute-start(f32[8,8,20,2]{2,1,3,0:T(8,128)S(1)} %copy.1015), channel_id=1, source_target_pairs={{0,1},{1,2},{2,3},{3,4},{4,5},{5,6},{6,7},{7,8},{8,9},{9,10},{10,1... | collective-permute-start | bytes 30728 | tf_op jit(solution)/shard_map/ppermute | solution.py:24
  142.4 3.9 %collective-permute-start.9 = (f32[8,8,20,2]{2,1,3,0:T(8,128)S(1)}, f32[8,8,20,2]{2,1,3,0:T(8,128)S(1)}, u32[]{:S(2)}, u32[]{:S(2)}) collective-permute-start(f32[8,8,20,2]{2,1,3,0:T(8,128)S(1)} %copy.1016), channel_id=1, source_target_pairs={{1,0},{2,1},{3,2},{4,3},{5,4},{6,5},{7,6},{8,7},{9,8},{10,9},{11,1... | collective-permute-start | bytes 30728 | tf_op jit(solution)/shard_map/ppermute | solution.py:27
  148.5 27.3 %copy-start.61 = (f32[8,19,132]{2,0,1:T(8,128)}, f32[8,19,132]{2,0,1:T(8,128)S(1)}, u32[]{:S(2)}) copy-start(f32[8,19,132]{2,0,1:T(8,128)S(1)} %get-tuple-element.122) | copy-start | bytes 240772
  149.2 26.7 %copy-start.151 = (f32[8,1,132]{2,0,1:T(8,128)}, f32[8,1,132]{2,0,1:T(8,128)S(1)}, u32[]{:S(2)}) copy-start(f32[8,1,132]{2,0,1:T(8,128)S(1)} %get-tuple-element.120) | copy-start | bytes 12676
  150.0 9.9 %copy-start.52 = (f32[8,20,131]{2,0,1:T(8,128)}, f32[8,20,131]{2,0,1:T(8,128)S(1)}, u32[]{:S(2)}) copy-start(f32[8,20,131]{2,0,1:T(8,128)S(1)} %get-tuple-element.158) | copy-start | bytes 251524
  150.8 20.0 %copy-start.29 = (f32[7,20,132]{2,0,1:T(8,128)}, f32[7,20,132]{2,0,1:T(8,128)S(1)}, u32[]{:S(2)}) copy-start(f32[7,20,132]{2,0,1:T(8,128)S(1)} %get-tuple-element.148) | copy-start | bytes 221764
  151.5 19.3 %copy-start.129 = (f32[1,20,132]{2,0,1:T(1,128)}, f32[1,20,132]{2,0,1:T(1,128)S(1)}, u32[]{:S(2)}) copy-start(f32[1,20,132]{2,0,1:T(1,128)S(1)} %get-tuple-element.146) | copy-start | bytes 31684
  152.2 11.0 %copy-start.27 = (f32[7,20,132]{2,0,1:T(8,128)}, f32[7,20,132]{2,0,1:T(8,128)S(1)}, u32[]{:S(2)}) copy-start(f32[7,20,132]{2,0,1:T(8,128)S(1)} %get-tuple-element.152) | copy-start | bytes 221764
  152.8 10.4 %copy-start.121 = (f32[1,20,132]{2,0,1:T(1,128)}, f32[1,20,132]{2,0,1:T(1,128)S(1)}, u32[]{:S(2)}) copy-start(f32[1,20,132]{2,0,1:T(1,128)S(1)} %get-tuple-element.150) | copy-start | bytes 31684
  154.4 8.8 %copy-start.54 = (f32[7,20,132]{2,0,1:T(8,128)}, f32[7,20,132]{2,0,1:T(8,128)S(1)}, u32[]{:S(2)}) copy-start(f32[7,20,132]{2,0,1:T(8,128)S(1)} %get-tuple-element.62) | copy-start | bytes 221764
  154.4 16.4 %copy-start.56 = (f32[7,20,132]{2,0,1:T(8,128)}, f32[7,20,132]{2,0,1:T(8,128)S(1)}, u32[]{:S(2)}) copy-start(f32[7,20,132]{2,0,1:T(8,128)S(1)} %get-tuple-element.61) | copy-start | bytes 221764
  155.4 15.3 %copy-start.4 = (f32[8,20,132]{2,0,1:T(8,128)}, f32[8,20,132]{2,0,1:T(8,128)S(1)}, u32[]{:S(2)}) copy-start(f32[8,20,132]{2,0,1:T(8,128)S(1)} %get-tuple-element.6) | copy-start | bytes 253444
  157.8 19.0 %copy-start.25 = (f32[8,20,131]{2,0,1:T(8,128)}, f32[8,20,131]{2,0,1:T(8,128)S(1)}, u32[]{:S(2)}) copy-start(f32[8,20,131]{2,0,1:T(8,128)S(1)} %get-tuple-element.136) | copy-start | bytes 251524
  157.9 19.0 %copy-start.36 = (f32[8,20,1]{2,0,1:T(8,128)}, f32[8,20,1]{2,0,1:T(8,128)S(1)}, u32[]{:S(2)}) copy-start(f32[8,20,1]{2,0,1:T(8,128)S(1)} %slice.655) | copy-start | bytes 1924
  160.9 16.0 %copy-start = (f32[8,20,132]{2,0,1:T(8,128)}, f32[8,20,132]{2,0,1:T(8,128)S(1)}, u32[]{:S(2)}) copy-start(f32[8,20,132]{2,0,1:T(8,128)S(1)} %get-tuple-element.13) | copy-start | bytes 253444
  160.9 16.0 %copy-start.13 = (f32[8,20,132]{2,0,1:T(8,128)}, f32[8,20,132]{2,0,1:T(8,128)S(1)}, u32[]{:S(2)}) copy-start(f32[8,20,132]{2,0,1:T(8,128)S(1)} %get-tuple-element.10) | copy-start | bytes 253444
  160.9 16.0 %copy-start.15 = (f32[8,20,132]{2,0,1:T(8,128)}, f32[8,20,132]{2,0,1:T(8,128)S(1)}, u32[]{:S(2)}) copy-start(f32[8,20,132]{2,0,1:T(8,128)S(1)} %get-tuple-element.11) | copy-start | bytes 253444
  160.9 16.0 %copy-start.17 = (f32[8,20,132]{2,0,1:T(8,128)}, f32[8,20,132]{2,0,1:T(8,128)S(1)}, u32[]{:S(2)}) copy-start(f32[8,20,132]{2,0,1:T(8,128)S(1)} %get-tuple-element.12) | copy-start | bytes 253444
  165.0 4.8 %copy-start.31 = (f32[8,20,132]{2,0,1:T(8,128)}, f32[8,20,132]{2,0,1:T(8,128)S(1)}, u32[]{:S(2)}) copy-start(f32[8,20,132]{2,0,1:T(8,128)S(1)} %fusion.45) | copy-start | bytes 253444
  167.0 6.1 %copy-start.9 = (f32[8,19,132]{2,0,1:T(8,128)}, f32[8,19,132]{2,0,1:T(8,128)S(1)}, u32[]{:S(2)}) copy-start(f32[8,19,132]{2,0,1:T(8,128)S(1)} %get-tuple-element.134) | copy-start | bytes 240772
  167.0 5.3 %copy-start.134 = (f32[8,1,132]{2,0,1:T(8,128)}, f32[8,1,132]{2,0,1:T(8,128)S(1)}, u32[]{:S(2)}) copy-start(f32[8,1,132]{2,0,1:T(8,128)S(1)} %get-tuple-element.132) | copy-start | bytes 12676
  167.7 8.1 %copy-start.11 = (f32[8,19,132]{2,0,1:T(8,128)}, f32[8,19,132]{2,0,1:T(8,128)S(1)}, u32[]{:S(2)}) copy-start(f32[8,19,132]{2,0,1:T(8,128)S(1)} %get-tuple-element.130) | copy-start | bytes 240772
  168.4 7.5 %copy-start.136 = (f32[8,1,132]{2,0,1:T(8,128)}, f32[8,1,132]{2,0,1:T(8,128)S(1)}, u32[]{:S(2)}) copy-start(f32[8,1,132]{2,0,1:T(8,128)S(1)} %get-tuple-element.128) | copy-start | bytes 12676
  170.8 5.9 %copy-start.2 = (f32[8,20,132]{2,0,1:T(8,128)}, f32[8,20,132]{2,0,1:T(8,128)S(1)}, u32[]{:S(2)}) copy-start(f32[8,20,132]{2,0,1:T(8,128)S(1)} %get-tuple-element.15) | copy-start | bytes 253444
  180.7 6.8 %copy-start.122 = (f32[1,20,132]{2,0,1:T(1,128)S(1)}, f32[1,20,132]{2,0,1:T(1,128)}, u32[]{:S(2)}) copy-start(f32[1,20,132]{2,0,1:T(1,128)} %copy-done.121) | copy-start | bytes 31684
  181.7 5.8 %copy-start.5 = (f32[8,20,132]{2,0,1:T(8,128)S(1)}, f32[8,20,132]{2,0,1:T(8,128)}, u32[]{:S(2)}) copy-start(f32[8,20,132]{2,0,1:T(8,128)} %copy-done.4) | copy-start | bytes 253444
  181.7 5.8 %copy-start.28 = (f32[7,20,132]{2,0,1:T(8,128)S(1)}, f32[7,20,132]{2,0,1:T(8,128)}, u32[]{:S(2)}) copy-start(f32[7,20,132]{2,0,1:T(8,128)} %copy-done.27) | copy-start | bytes 221764
  181.7 5.8 %copy-start.55 = (f32[7,20,132]{2,0,1:T(8,128)S(1)}, f32[7,20,132]{2,0,1:T(8,128)}, u32[]{:S(2)}) copy-start(f32[7,20,132]{2,0,1:T(8,128)} %copy-done.54) | copy-start | bytes 221764
  196.4 5.0 %copy-start.75 = (f32[8,20,1]{2,0,1:T(8,128)S(1)}, f32[8,20,1]{2,0,1:T(8,128)}, u32[]{:S(2)}) copy-start(f32[8,20,1]{2,0,1:T(8,128)} %copy-done.74) | copy-start | bytes 1924
  196.4 5.7 %copy-start.65 = (f32[8,20,1]{2,0,1:T(8,128)S(1)}, f32[8,20,1]{2,0,1:T(8,128)}, u32[]{:S(2)}) copy-start(f32[8,20,1]{2,0,1:T(8,128)} %copy-done.63) | copy-start | bytes 1924
  197.3 8.7 %copy-start.70 = (f32[8,20,132]{2,0,1:T(8,128)S(1)}, f32[8,20,132]{2,0,1:T(8,128)}, u32[]{:S(2)}) copy-start(f32[8,20,132]{2,0,1:T(8,128)} %get-tuple-element.50) | copy-start | bytes 253444
  197.3 10.2 %copy-start.72 = (f32[8,20,132]{2,0,1:T(8,128)S(1)}, f32[8,20,132]{2,0,1:T(8,128)}, u32[]{:S(2)}) copy-start(f32[8,20,132]{2,0,1:T(8,128)} %get-tuple-element.68) | copy-start | bytes 253444
  197.3 12.5 %copy-start.40 = (f32[8,20,132]{2,0,1:T(8,128)S(1)}, f32[8,20,132]{2,0,1:T(8,128)}, u32[]{:S(2)}) copy-start(f32[8,20,132]{2,0,1:T(8,128)} %copy-done.39) | copy-start | bytes 253444
  198.0 14.2 %copy-start.32 = (f32[8,20,132]{2,0,1:T(8,128)S(1)}, f32[8,20,132]{2,0,1:T(8,128)}, u32[]{:S(2)}) copy-start(f32[8,20,132]{2,0,1:T(8,128)} %copy-done.31) | copy-start | bytes 253444
  198.7 14.2 %copy-start.46 = (f32[8,20,132]{2,0,1:T(8,128)S(1)}, f32[8,20,132]{2,0,1:T(8,128)}, u32[]{:S(2)}) copy-start(f32[8,20,132]{2,0,1:T(8,128)} %copy-done.45) | copy-start | bytes 253444
  200.7 13.5 %copy-start.68 = (f32[8,20,132]{2,0,1:T(8,128)S(1)}, f32[8,20,132]{2,0,1:T(8,128)}, u32[]{:S(2)}) copy-start(f32[8,20,132]{2,0,1:T(8,128)} %get-tuple-element.9) | copy-start | bytes 253444
  207.5 10.5 %copy-start.71 = (f32[8,20,132]{2,0,1:T(8,128)S(1)}, f32[8,20,132]{2,0,1:T(8,128)}, u32[]{:S(2)}) copy-start(f32[8,20,132]{2,0,1:T(8,128)} %get-tuple-element.5) | copy-start | bytes 253444
  208.2 11.1 %copy-start.77 = (f32[8,20,1]{2,0,1:T(8,128)S(1)}, f32[8,20,1]{2,0,1:T(8,128)}, u32[]{:S(2)}) copy-start(f32[8,20,1]{2,0,1:T(8,128)} %copy-done.76) | copy-start | bytes 1924
  208.2 11.2 %slice-start.1 = ((f32[8,20,132]{2,0,1:T(8,128)}), f32[8,20,1]{2,0,1:T(8,128)S(1)}, s32[]{:S(2)}) async-start(f32[8,20,132]{2,0,1:T(8,128)} %copy-done.39), calls=%async_computation.1 | async-start | bytes 163840 | tf_op jit(solution)/shard_map/jit(_roll_static)/slice | solution.py:33
  209.8 11.2 %copy-start.117 = (f32[8,20,1]{2,0,1:T(8,128)S(1)}, f32[8,20,1]{2,0,1:T(8,128)}, u32[]{:S(2)}) copy-start(f32[8,20,1]{2,0,1:T(8,128)} %slice.695) | copy-start | bytes 1924
  211.1 10.9 %copy-start.118 = (f32[8,20,1]{2,0,1:T(8,128)S(1)}, f32[8,20,1]{2,0,1:T(8,128)}, u32[]{:S(2)}) copy-start(f32[8,20,1]{2,0,1:T(8,128)} %slice.675) | copy-start | bytes 1924
  212.1 10.7 %copy-start.119 = (f32[8,20,1]{2,0,1:T(8,128)S(1)}, f32[8,20,1]{2,0,1:T(8,128)}, u32[]{:S(2)}) copy-start(f32[8,20,1]{2,0,1:T(8,128)} %slice.660) | copy-start | bytes 1924
  212.1 11.6 %copy-start.163 = (f32[8,20,1]{1,0,2:T(8,128)S(1)}, f32[8,20,1]{1,0,2:T(8,128)}, u32[]{:S(2)}) copy-start(f32[8,20,1]{1,0,2:T(8,128)} %copy.1041) | copy-start | bytes 1924
  212.9 11.6 %copy-start.164 = (f32[8,20,1]{1,0,2:T(8,128)S(1)}, f32[8,20,1]{1,0,2:T(8,128)}, u32[]{:S(2)}) copy-start(f32[8,20,1]{1,0,2:T(8,128)} %copy.1037) | copy-start | bytes 1924
  212.9 12.4 %copy-start.165 = (f32[8,20,1]{1,0,2:T(8,128)S(1)}, f32[8,20,1]{1,0,2:T(8,128)}, u32[]{:S(2)}) copy-start(f32[8,20,1]{1,0,2:T(8,128)} %copy.1026) | copy-start | bytes 1924
  212.9 13.2 %copy-start.166 = (f32[8,20,1]{1,0,2:T(8,128)S(1)}, f32[8,20,1]{1,0,2:T(8,128)}, u32[]{:S(2)}) copy-start(f32[8,20,1]{1,0,2:T(8,128)} %copy.1033) | copy-start | bytes 1924
  212.9 13.9 %copy-start.167 = (f32[8,20,1]{1,0,2:T(8,128)S(1)}, f32[8,20,1]{1,0,2:T(8,128)}, u32[]{:S(2)}) copy-start(f32[8,20,1]{1,0,2:T(8,128)} %copy.1035) | copy-start | bytes 1924
  213.6 14.0 %copy-start.168 = (f32[8,20,1]{1,0,2:T(8,128)S(1)}, f32[8,20,1]{1,0,2:T(8,128)}, u32[]{:S(2)}) copy-start(f32[8,20,1]{1,0,2:T(8,128)} %copy.1056) | copy-start | bytes 1924
  213.6 14.8 %copy-start.120 = (f32[8,20,1]{2,0,1:T(8,128)S(1)}, f32[8,20,1]{2,0,1:T(8,128)}, u32[]{:S(2)}) copy-start(f32[8,20,1]{2,0,1:T(8,128)} %slice.684) | copy-start | bytes 1924
  214.2 16.6 %slice-start = ((f32[8,20,132]{2,0,1:T(8,128)}), f32[8,20,1]{2,0,1:T(8,128)S(1)}, s32[]{:S(2)}) async-start(f32[8,20,132]{2,0,1:T(8,128)} %copy-done.31), calls=%async_computation | async-start | bytes 163840 | tf_op jit(solution)/shard_map/jit(_roll_static)/slice | solution.py:33
  216.6 16.8 %copy-start.7 = (f32[1,8,19,132]{3,1,2,0:T(8,128)S(1)}, f32[1,8,19,132]{3,1,2,0:T(8,128)}, u32[]{:S(2)}) copy-start(f32[1,8,19,132]{3,1,2,0:T(8,128)} %get-tuple-element.133) | copy-start | bytes 240772
  216.6 16.8 %copy-start.8 = (f32[1,8,19,132]{3,1,2,0:T(8,128)S(1)}, f32[1,8,19,132]{3,1,2,0:T(8,128)}, u32[]{:S(2)}) copy-start(f32[1,8,19,132]{3,1,2,0:T(8,128)} %get-tuple-element.129) | copy-start | bytes 240772
  216.6 16.8 %copy-start.131 = (f32[1,1,20,132]{3,1,2,0:T(1,128)S(1)}, f32[1,1,20,132]{3,1,2,0:T(1,128)}, u32[]{:S(2)}) copy-start(f32[1,1,20,132]{3,1,2,0:T(1,128)} %get-tuple-element.145) | copy-start | bytes 31684
  216.6 16.8 %copy-start.133 = (f32[1,8,1,132]{3,1,2,0:T(8,128)S(1)}, f32[1,8,1,132]{3,1,2,0:T(8,128)}, u32[]{:S(2)}) copy-start(f32[1,8,1,132]{3,1,2,0:T(8,128)} %get-tuple-element.127) | copy-start | bytes 12676
  (117 other events, 235.1 us)
where the time goes:
time: 246 us
  waiting for transfers between devices  98.8 us (40%)
  local copies, waits for them, and re-layouts  83.3 us (34%)
  starting transfers between devices  39.2 us (16%)
  other arithmetic  22.4 us (9%)
    ppermute x6, waiting for transfers between devices, passed_along(): return lax.ppermute(value, axis, pairs)  93.4 us
    concatenate x43, local copies, waits for them, and re-layouts, next_cell(): return jnp.roll(values, -1, axis_of[direc])  32.2 us
    concatenate x38, local copies, waits for them, and re-layouts, prev_cell(): return jnp.roll(values, 1, axis_of[direc])  24.7 us
    ppermute x2, starting transfers between devices, with_halo(): lax.ppermute(lax.slice_in_dim(block, block.shape[dim] - width, None, axis...  24.4 us
    slice x19, local copies, waits for them, and re-layouts, prev_cell(): return jnp.roll(values, 1, axis_of[direc])  10.2 us
    ppermute x6, starting transfers between devices, passed_along(): return lax.ppermute(value, axis, pairs)  9.67 us
    unnamed x7, other arithmetic  6.61 us
    slice x18, local copies, waits for them, and re-layouts, next_cell(): return jnp.roll(values, -1, axis_of[direc])  5.15 us
  transfers between devices with their start and end apart: 10, of which 9 were waited for; matrix products, arithmetic and copies ran while one was open for 1% of the time, Pallas kernels for 0%

commit v1 on v0

v1 whole, which is shorter than its diff:
```python
import functools
import jax
import jax.numpy as jnp
from jax import lax
from jax.experimental import pallas as pl
from jax.experimental.pallas import tpu as pltpu
from jax.sharding import PartitionSpec as P

HALF_DT = 0.025
EDGE = 0.125


def turned(x, amount, axis):
    return pltpu.roll(x, amount % x.shape[axis], axis)


def cell_terms(w, c):
    rho, m0, m1, m2, _, _, _, tracer = w
    inv = 1.0 / rho
    v = [m0 * inv, m1 * inv, m2 * inv]
    m = [m0, m1, m2]
    sq = [c[0] * c[0], c[1] * c[1], c[2] * c[2]]
    return dict(rho=rho, m=m, c=c, s=tracer, inv=inv, v=v, sq=sq)


def side(t, d):
    j, k = [i for i in range(3) if i != d]
    vd = t["v"][d]
    return [
        t["rho"], t["m"][0], t["m"][1], t["m"][2], t["c"][j], t["c"][k], t["s"],
        t["inv"], t["v"][0], t["v"][1], t["v"][2], t["sq"][j] + t["sq"][k],
        t["m"][0] * vd, t["m"][1] * vd, t["m"][2] * vd,
        vd * t["c"][j], vd * t["c"][k], t["s"] * vd,
    ]


def face_flux(left, right, n, d):
    j, k = [i for i in range(3) if i != d]
    nn = n * n
    vl, vr = left[8 + d], right[8 + d]
    pl_, pr = nn + left[11], nn + right[11]
    signal = jnp.maximum(
        jnp.abs(vl) + jnp.sqrt(1.0 + pl_ * left[7]), jnp.abs(vr) + jnp.sqrt(1.0 + pr * right[7])
    )
    total = [left[i] + right[i] for i in range(18)]
    jump = [right[i] - left[i] for i in range(7)]
    mass = total[1 + d] - signal * jump[0]
    mom = [None] * 3
    mom[d] = total[12 + d] - 2.0 * nn + total[0] + 0.5 * (pl_ + pr) - signal * jump[1 + d]
    mom[j] = total[12 + j] - n * total[4] - signal * jump[1 + j]
    mom[k] = total[12 + k] - n * total[5] - signal * jump[1 + k]
    ind = [None] * 3
    ind[j] = total[15] - n * total[8 + j] - signal * jump[4]
    ind[k] = total[16] - n * total[8 + k] - signal * jump[5]
    tracer = total[17] - signal * jump[6]
    return [mass] + mom + [tracer], ind


def packed_advance(w, nxt, prv):
    b = w[4:7]
    c = [0.5 * (b[d] + nxt[d](b[d])) for d in range(3)]
    t = cell_terms(w, c)
    flow, ind = [], []
    for d in range(3):
        right = side(t, d)
        left = [prv[d](x) for x in right]
        f, g = face_flux(left, right, b[d], d)
        flow.append(f)
        ind.append(g)
    e2 = EDGE * (ind[1][0] + prv[0](ind[1][0]) - (ind[0][1] + prv[1](ind[0][1])))
    e0 = EDGE * (ind[2][1] + prv[1](ind[2][1]) - (ind[1][2] + prv[2](ind[1][2])))
    e1 = EDGE * (ind[0][2] + prv[2](ind[0][2]) - (ind[2][0] + prv[0](ind[2][0])))
    out = []
    for i, q in enumerate([w[0], w[1], w[2], w[3], w[7]]):
        div = nxt[0](flow[0][i]) - flow[0][i]
        for d in (1, 2):
            div = div + (nxt[d](flow[d][i]) - flow[d][i])
        out.append(q - HALF_DT * div)
    dt = 2.0 * HALF_DT
    f0 = b[0] - dt * (nxt[1](e2) - e2 - (nxt[2](e1) - e1))
    f1 = b[1] - dt * (nxt[2](e0) - e0 - (nxt[0](e2) - e2))
    f2 = b[2] - dt * (nxt[0](e1) - e1 - (nxt[1](e0) - e0))
    return [out[0], out[1], out[2], out[3], f0, f1, f2, out[4]]


def step_kernel(rows, rows_ref, low_ref, high_ref, out_ref, edge_ref):
    lane = lax.broadcasted_iota(jnp.int32, (8, 128), 1)
    sub = lane % 8
    nxt = [lambda x: turned(x, -8, 1), lambda x: turned(x, -1, 1), lambda x: turned(x, -1, 0)]
    prv = [lambda x: turned(x, 8, 1), lambda x: turned(x, 1, 1), lambda x: turned(x, 1, 0)]

    def fields(q, f):
        return rows_ref[q, f * 8:(f + 1) * 8, :]

    bases = [0, rows + 3 - 16]
    for tile, base in enumerate(bases):
        w = []
        for f in range(8):
            low, high = low_ref[f * 8:(f + 1) * 8, :], high_ref[f * 8:(f + 1) * 8, :]
            acc = jnp.ones((8, 128), jnp.float32)
            for g in range(16):
                q = base + g
                x = fields(q, f)
                here = lane // 8 == g
                a = jnp.where(sub < 4, turned(x, 8 * g + 1, 1), turned(x, 8 * g + 4 - 126, 1))
                a = jnp.where(sub == 0, turned(low, 8 * g - 2 * q - 1, 1), a)
                a = jnp.where(sub > 5, turned(high, 8 * g + 6 - 2 * q, 1), a)
                acc = jnp.where(here, a, acc)
            w.append(acc)
        for f, x in enumerate(packed_advance(w, nxt, prv)):
            edge_ref[tile, f * 8:(f + 1) * 8, :] = x

    az_n, az_p = nxt[1], prv[1]
    k_n, k_p = nxt[2], prv[2]

    def row_part(q):
        w = [fields(q, f) for f in range(8)]
        beyond = pltpu.roll(high_ref[40:48, :], lax.rem(127 - 2 * q + 128, 128), 1)
        after = jnp.where(lane == 127, beyond, az_n(w[5]))
        c = [0.5 * (w[4] + fields(q + 1, 4)), 0.5 * (w[5] + after), 0.5 * (w[6] + k_n(w[6]))]
        t = cell_terms(w, c)
        r1, r2 = side(t, 1), side(t, 2)
        flow1, ind1 = face_flux([az_p(x) for x in r1], r1, w[5], 1)
        flow2, ind2 = face_flux([k_p(x) for x in r2], r2, w[6], 2)
        return w, t, flow1, ind1, flow2, ind2

    def fresh(q):
        w, t, flow1, ind1, flow2, ind2 = row_part(q)
        return w, side(t, 0), flow1, ind1, flow2, ind2

    _, left, _, ind1, _, ind2 = fresh(jnp.int32(0))
    zero = jnp.zeros((8, 128), jnp.float32)
    start = tuple(left) + (ind1[0], ind2[0]) + (zero,) * 9

    def body(q, carry):
        left, p10, p20 = carry[:18], carry[18], carry[19]
        partial, part_b = carry[20:25], carry[25:28]
        pending_e2 = carry[28]
        w, right, flow1, ind1, flow2, ind2 = fresh(q)
        flow0, ind0 = face_flux(left, right, w[4], 0)
        e2 = EDGE * (ind1[0] + p10 - (ind0[1] + az_p(ind0[1])))
        e1 = EDGE * (ind0[2] + k_p(ind0[2]) - (ind2[0] + p20))
        e0 = EDGE * (ind2[1] + az_p(ind2[1]) - (ind1[2] + k_p(ind1[2])))
        dt = 2.0 * HALF_DT

        done = [partial[i] - HALF_DT * flow0[i] for i in range(5)]
        done_b = [part_b[0], part_b[1] + dt * e2, part_b[2] - dt * e1]
        fin = [done[0], done[1], done[2], done[3], done_b[0], done_b[1], done_b[2], done[4]]

        @pl.when(q >= 2)
        def _():
            r = q - 2
            second = (q - 1 >= 14).astype(jnp.int32)
            g = q - 1 - second * bases[1]
            for f in range(8):
                e = edge_ref[second, f * 8:(f + 1) * 8, :]
                val = jnp.where(lane == 0, pltpu.roll(e, lax.rem(128 + 127 - 8 * g, 128), 1), fin[f])
                val = jnp.where(lane == 127, pltpu.roll(e, lax.rem(128 + 122 - 8 * g, 128), 1), val)
                out_ref[pl.ds(f * 8 * rows + r, 8, stride=rows), :] = val

        new = []
        cells = [w[0], w[1], w[2], w[3], w[7]]
        for i in range(5):
            div = (az_n(flow1[i]) - flow1[i]) + (k_n(flow2[i]) - flow2[i]) - flow0[i]
            new.append(cells[i] - HALF_DT * div)
        n0 = w[4] - dt * (az_n(e2) - e2 - (k_n(e1) - e1))
        n1 = w[5] - dt * (k_n(e0) - e0 + e2)
        n2 = w[6] - dt * (-e1 - (az_n(e0) - e0))
        return tuple(right) + (ind1[0], ind2[0]) + tuple(new) + (n0, n1, n2, e2)

    lax.fori_loop(1, rows + 2, body, start)


def step(rows_form, low, high):
    q, _, width = rows_form.shape
    rows = q - 3
    out = pl.pallas_call(
        functools.partial(step_kernel, rows),
        out_shape=jax.ShapeDtypeStruct((64 * rows, width), jnp.float32),
        in_specs=[pl.BlockSpec(memory_space=pltpu.VMEM)] * 3,
        out_specs=pl.BlockSpec(memory_space=pltpu.VMEM),
        scratch_shapes=[pltpu.VMEM((2, 64, width), jnp.float32)],
        name="advance_rows",
    )(rows_form, low, high)
    return out.reshape(8, 8, rows, width)


def passed_along(value, axis, steps):
    count = lax.axis_size(axis)
    pairs = [(source, (source + steps) % count) for source in range(count)]
    return lax.ppermute(value, axis, pairs)


def with_halo(block, sides, width, periodic):
    for axis, dim in sides:
        count = lax.axis_size(axis)
        forward = [(i, i + 1) for i in range(count - 1)]
        if periodic:
            forward.append((count - 1, 0))
        backward = [(target, source) for source, target in forward]
        low = lax.ppermute(
            lax.slice_in_dim(block, block.shape[dim] - width, None, axis=dim), axis, forward
        )
        high = lax.ppermute(lax.slice_in_dim(block, 0, width, axis=dim), axis, backward)
        block = jnp.concatenate([low, block, high], axis=dim)
    return block


def outflow(padded, place, last_place):
    inner = padded[:, :, 2:-2]
    lower = jnp.where(
        place == 0, jnp.broadcast_to(inner[:, :, :1], padded[:, :, :2].shape), padded[:, :, :2]
    )
    upper = jnp.where(
        place == last_place,
        jnp.broadcast_to(inner[:, :, -1:], padded[:, :, -2:].shape),
        padded[:, :, -2:],
    )
    return jnp.concatenate([lower, inner, upper], axis=2)


def rotate_local(values, amount):
    row_width = values.shape[-1]
    last_axis = values.ndim - 1
    for bit_level in range((row_width - 1).bit_length()):
        rolled = jnp.roll(values, 1 << bit_level, axis=last_axis)
        chosen = amount // (1 << bit_level) % 2 == 1
        values = jnp.where(chosen[:, None], rolled, values)
    return values


def per_device(state, shift):
    row_count = state.shape[2]
    col_count = state.shape[3]
    column = lax.broadcasted_iota(jnp.int32, (row_count, col_count), 1)
    residual = shift % col_count
    coarse = shift // col_count
    rolled = rotate_local(state, residual)
    carried = passed_along(rolled, "az", 1)
    remapped = jnp.where((column >= residual[:, None])[None, None], rolled, carried)
    for bit_level in range((lax.axis_size("az") - 1).bit_length()):
        arrived = passed_along(remapped, "az", 1 << bit_level)
        chosen = coarse // (1 << bit_level) % 2 == 1
        remapped = jnp.where(chosen[None, None, :, None], arrived, remapped)
    place = lax.axis_index("rad")
    last_place = lax.axis_size("rad") - 1
    radial = with_halo(remapped, (("rad", 2),), 2, False)
    radial = outflow(radial, place, last_place)[:, :, 1:]
    rows_form = radial.transpose(2, 0, 1, 3).reshape(row_count + 3, 64, col_count)

    def edge(cells, steps):
        flat = cells.reshape(64, 2 * (row_count + 3))
        flat = jnp.pad(flat, ((0, 0), (0, col_count - flat.shape[1])))
        return passed_along(flat, "az", steps)

    low = edge(radial[..., -2:], 1)
    high = edge(radial[..., :2], -1)
    return step(rows_form, low, high)


def solution(mesh):
    placed = (P(None, None, "rad", "az"), P("rad"))
    return jax.shard_map(
        per_device,
        mesh=mesh,
        in_specs=placed,
        out_specs=P(None, None, "rad", "az"),
        check_vma=False,
    )
```

time: 246 us -> 155 us (0.63)
  local copies, waits for them, and re-layouts: 83.3 us -> 4.98 us
  other arithmetic: 22.4 us -> 3.18 us
  Pallas kernels: 0 us -> 9.17 us
  starting transfers between devices: 39.2 us -> 34.1 us
  waiting for transfers between devices: 98.8 us -> 103 us
    concatenate x81 -> x0, local copies, waits for them, and re-layouts: 56.9 us -> none  [the longest x43 32.2 us: next_cell(): return jnp.roll(values, -1, axis_of[direc])]
    ppermute x2 -> x1, starting transfers between devices: 24.4 us -> 1.92 us  [with_halo(): lax.ppermute(lax.slice_in_dim(block, block.shape[dim] - width, None, axis...]
    ppermute x6 -> x8, starting transfers between devices: 9.67 us -> 27.4 us  [passed_along(): return lax.ppermute(value, axis, pairs)]
    slice x40 -> x2, local copies, waits for them, and re-layouts: 17.2 us -> 0.34 us  [the longest x1 0.29 us: per_device(): high = edge(radial[..., :2], -1)]
    sub x16 -> x0, other arithmetic: 10.8 us -> none  [the longest x6 3.93 us: rusanov(): 0.5 * (left[2][k] + right[2][k])]
    pallas_call x0 -> x1, Pallas kernels: none -> 9.17 us  [step(): pl.pallas_call(functools.partial(step_kernel, rows), out_shape=jax.ShapeD...]
    unnamed x7 -> x0, other arithmetic: 6.61 us -> none
    ppermute x6 -> x8, waiting for transfers between devices: 93.4 us -> 99.8 us  [passed_along(): return lax.ppermute(value, axis, pairs)]
  transfers between devices with their start and end apart: 10 -> 10, of which waited for: 9 -> 8; matrix products, arithmetic and copies ran while one was open for 1% -> 1% of each run, Pallas kernels for 0% -> 0%
where the time goes in v1:
time: 155 us
  waiting for transfers between devices  103 us (66%)
  starting transfers between devices  34.1 us (22%)
  Pallas kernels  9.17 us (6%)
  local copies, waits for them, and re-layouts  4.98 us (3%)
  other arithmetic  3.18 us (2%)
    ppermute x8, waiting for transfers between devices, passed_along(): return lax.ppermute(value, axis, pairs)  99.8 us
    ppermute x8, starting transfers between devices, passed_along(): return lax.ppermute(value, axis, pairs)  27.4 us
    pallas_call x1, Pallas kernels, step(): pl.pallas_call(functools.partial(step_kernel, rows), out_shape=jax.ShapeD...  9.17 us
    ppermute x1, starting transfers between devices, with_halo(): lax.ppermute(lax.slice_in_dim(block, 0, width, axis=dim), axis, backward)  4.87 us
    ppermute x1, waiting for transfers between devices, with_halo(): lax.ppermute(lax.slice_in_dim(block, 0, width, axis=dim), axis, backward)  3.23 us
  transfers between devices with their start and end apart: 10, of which 8 were waited for; matrix products, arithmetic and copies ran while one was open for 1% of the time, Pallas kernels for 0%

profile of v1, /device:TPU:109, one launch (start us, length us, event | category | flops | bytes accessed | tf_op | source)
XLA Modules:
  0.0 154.8 jit_solution(1629493745977970682)
XLA Ops:
  0.0 0.7 fusion
  0.7 0.0 copy-start
  0.7 1.3 slice.79
  2.0 0.0 copy-done
  2.0 0.2 maximum_select_fusion
  2.3 0.2 slice.100
  2.5 0.2 maximum_select_fusion.1
  2.7 0.2 slice.102
  2.9 0.2 maximum_select_fusion.2
  3.1 0.2 slice.104
  3.3 0.2 maximum_select_fusion.3
  3.5 0.2 slice.106
  3.7 0.2 maximum_select_fusion.4
  3.9 0.2 slice.108
  4.1 0.2 maximum_select_fusion.5
  4.3 0.2 fusion.25
  4.5 0.2 maximum_select_fusion.6
  4.8 1.6 %collective-permute-start = (f32[8,8,16,128]{3,2,1,0:T(8,128)S(1)}, f32[8,8,16,128]{3,2,1,0:T(8,128)S(1)}, u32[]{:S(2)}, u32[]{:S(2)}) collective-permute-start(f32[8,8,16,128]{3,2,1,0:T(8,128)S(1)} %maximum_select_fusion.6), channel_id=1, source_target_pairs={{0,1},{1,2},{2,3},{3,4},{4,5},{5,6},{6,7},{7,8},{8,9},{9,10},{10,1... | collective-permute-start | bytes 1572872 | tf_op jit(solution)/shard_map/ppermute | solution.py:191
  6.3 0.1 iota_compare_fusion
  6.4 6.1 %collective-permute-done = f32[8,8,16,128]{3,2,1,0:T(8,128)S(1)} collective-permute-done((f32[8,8,16,128]{3,2,1,0:T(8,128)S(1)}, f32[8,8,16,128]{3,2,1,0:T(8,128)S(1)}, u32[]{:S(2)}, u32[]{:S(2)}) %collective-permute-start) | collective-permute-done | bytes 524320 | tf_op jit(solution)/shard_map/ppermute | solution.py:191
  12.4 0.1 broadcast_select_fusion.5
  12.5 2.6 %collective-permute-start.1 = (f32[8,8,16,128]{3,2,1,0:T(8,128)S(1)}, f32[8,8,16,128]{3,2,1,0:T(8,128)S(1)}, u32[]{:S(2)}, u32[]{:S(2)}) collective-permute-start(f32[8,8,16,128]{3,2,1,0:T(8,128)S(1)} %broadcast_select_fusion.5), channel_id=1, source_target_pairs={{0,1},{1,2},{2,3},{3,4},{4,5},{5,6},{6,7},{7,8},{8,9},{9,10},{10,1... | collective-permute-start | bytes 1572872 | tf_op jit(solution)/shard_map/ppermute | solution.py:191
  15.1 6.1 %collective-permute-done.1 = f32[8,8,16,128]{3,2,1,0:T(8,128)S(1)} collective-permute-done((f32[8,8,16,128]{3,2,1,0:T(8,128)S(1)}, f32[8,8,16,128]{3,2,1,0:T(8,128)S(1)}, u32[]{:S(2)}, u32[]{:S(2)}) %collective-permute-start.1) | collective-permute-done | bytes 524320 | tf_op jit(solution)/shard_map/ppermute | solution.py:191
  21.2 0.1 broadcast_select_fusion
  21.3 5.3 %collective-permute-start.2 = (f32[8,8,16,128]{3,2,1,0:T(8,128)S(1)}, f32[8,8,16,128]{3,2,1,0:T(8,128)S(1)}, u32[]{:S(2)}, u32[]{:S(2)}) collective-permute-start(f32[8,8,16,128]{3,2,1,0:T(8,128)S(1)} %broadcast_select_fusion), channel_id=1, source_target_pairs={{0,2},{1,3},{2,4},{3,5},{4,6},{5,7},{6,8},{7,9},{8,10},{9,11},{10,... | collective-permute-start | bytes 1572872 | tf_op jit(solution)/shard_map/ppermute | solution.py:191
  26.6 10.2 %collective-permute-done.2 = f32[8,8,16,128]{3,2,1,0:T(8,128)S(1)} collective-permute-done((f32[8,8,16,128]{3,2,1,0:T(8,128)S(1)}, f32[8,8,16,128]{3,2,1,0:T(8,128)S(1)}, u32[]{:S(2)}, u32[]{:S(2)}) %collective-permute-start.2) | collective-permute-done | bytes 524320 | tf_op jit(solution)/shard_map/ppermute | solution.py:191
  36.8 0.1 broadcast_select_fusion.1
  36.9 0.1 collective-permute-start.3
  37.0 13.6 %collective-permute-done.3 = f32[8,8,16,128]{3,2,1,0:T(8,128)S(1)} collective-permute-done((f32[8,8,16,128]{3,2,1,0:T(8,128)S(1)}, f32[8,8,16,128]{3,2,1,0:T(8,128)S(1)}, u32[]{:S(2)}, u32[]{:S(2)}) %collective-permute-start.3) | collective-permute-done | bytes 524320 | tf_op jit(solution)/shard_map/ppermute | solution.py:191
  50.7 0.1 broadcast_select_fusion.2
  50.8 0.1 collective-permute-start.4
  50.9 36.4 %collective-permute-done.4 = f32[8,8,16,128]{3,2,1,0:T(8,128)S(1)} collective-permute-done((f32[8,8,16,128]{3,2,1,0:T(8,128)S(1)}, f32[8,8,16,128]{3,2,1,0:T(8,128)S(1)}, u32[]{:S(2)}, u32[]{:S(2)}) %collective-permute-start.4) | collective-permute-done | bytes 524320 | tf_op jit(solution)/shard_map/ppermute | solution.py:191
  87.3 0.1 broadcast_select_fusion.3
  87.4 0.1 collective-permute-start.5
  87.5 25.2 %collective-permute-done.5 = f32[8,8,16,128]{3,2,1,0:T(8,128)S(1)} collective-permute-done((f32[8,8,16,128]{3,2,1,0:T(8,128)S(1)}, f32[8,8,16,128]{3,2,1,0:T(8,128)S(1)}, u32[]{:S(2)}, u32[]{:S(2)}) %collective-permute-start.5) | collective-permute-done | bytes 524320 | tf_op jit(solution)/shard_map/ppermute | solution.py:191
  112.7 0.1 broadcast_select_fusion.4
  112.9 1.9 %collective-permute-start.6 = (f32[8,8,2,128]{3,2,1,0:T(2,128)S(1)}, f32[8,8,2,128]{3,2,1,0:T(2,128)S(1)}, u32[]{:S(2)}, u32[]{:S(2)}) collective-permute-start(f32[8,8,2,128]{3,2,1,0:T(2,128)S(1)} %get-tuple-element.13), channel_id=1, source_target_pairs={{0,32},{32,64},{64,96},{96,128},{128,160},{160,192},{192,224},{1,3... | collective-permute-start | bytes 196616 | tf_op jit(solution)/shard_map/ppermute | solution.py:201
  114.9 4.9 %collective-permute-start.7 = (f32[8,8,2,128]{3,2,1,0:T(2,128)S(1)}, f32[8,8,2,128]{3,2,1,0:T(2,128)S(1)}, u32[]{:S(2)}, u32[]{:S(2)}) collective-permute-start(f32[8,8,2,128]{3,2,1,0:T(2,128)S(1)} %get-tuple-element.14), channel_id=1, source_target_pairs={{32,0},{64,32},{96,64},{128,96},{160,128},{192,160},{224,192},{33,... | collective-permute-start | bytes 196616 | tf_op jit(solution)/shard_map/ppermute | solution.py:204
  119.8 0.0 collective-permute-done.6
  119.8 3.2 %collective-permute-done.7 = f32[8,8,2,128]{3,2,1,0:T(2,128)S(1)} collective-permute-done((f32[8,8,2,128]{3,2,1,0:T(2,128)S(1)}, f32[8,8,2,128]{3,2,1,0:T(2,128)S(1)}, u32[]{:S(2)}, u32[]{:S(2)}) %collective-permute-start.7) | collective-permute-done | bytes 65568 | tf_op jit(solution)/shard_map/ppermute | solution.py:204
  123.1 0.1 pad_maximum_fusion
  123.2 0.3 fusion.22
  123.5 0.2 reshape.36
  123.8 17.6 %collective-permute-start.8 = (f32[64,128]{1,0:T(8,128)S(1)}, f32[64,128]{1,0:T(8,128)S(1)}, u32[]{:S(2)}, u32[]{:S(2)}) collective-permute-start(f32[64,128]{1,0:T(8,128)S(1)} %pad.7), channel_id=1, source_target_pairs={{0,1},{1,2},{2,3},{3,4},{4,5},{5,6},{6,7},{7,8},{8,9},{9,10},{10,1... | collective-permute-start | bytes 98312 | tf_op jit(solution)/shard_map/ppermute | solution.py:191
  141.4 0.2 reshape.37
  141.6 0.1 collective-permute-start.9
  141.7 0.1 slice_bitcast_fusion
  141.8 0.9 copy.12
  142.7 0.0 collective-permute-done.8.low_ref
  142.7 0.0 copy-start.1
  142.7 2.3 %collective-permute-done.9.high_ref = f32[64,128]{1,0:T(8,128)S(1)} collective-permute-done((f32[64,128]{1,0:T(8,128)S(1)}, f32[64,128]{1,0:T(8,128)S(1)}, u32[]{:S(2)}, u32[]{:S(2)}) %collective-permute-start.9) | collective-permute-done | bytes 32800 | tf_op jit(solution)/shard_map/ppermute | solution.py:191
  145.0 0.0 copy-start.2
  145.0 0.0 copy-done.1
  145.0 0.6 copy-done.2
  145.6 9.2 %advance_rows.1 = f32[1024,128]{1,0:T(8,128)} custom-call(f32[19,64,128]{2,1,0:T(8,128)} %bitcast.20, f32[64,128]{1,0:T(8,128)} %copy-done.1, f32[64,128]{1,0:T(8,128)} %copy-done.2), custom_call_target="tpu_custom_call" | custom-call | tf_op jit(solution)/shard_map/advance_rows/pallas_call | solution.py:177
  (8 shorter events, 0.2 us)
Async XLA Ops:
  0.7 1.3 copy-start
  4.8 7.7 %collective-permute-start = (f32[8,8,16,128]{3,2,1,0:T(8,128)S(1)}, f32[8,8,16,128]{3,2,1,0:T(8,128)S(1)}, u32[]{:S(2)}, u32[]{:S(2)}) collective-permute-start(f32[8,8,16,128]{3,2,1,0:T(8,128)S(1)} %maximum_select_fusion.6), channel_id=1, source_target_pairs={{0,1},{1,2},{2,3},{3,4},{4,5},{5,6},{6,7},{7,8},{8,9},{9,10},{10,1... | collective-permute-start | bytes 1572872 | tf_op jit(solution)/shard_map/ppermute | solution.py:191
  12.5 8.7 %collective-permute-start.1 = (f32[8,8,16,128]{3,2,1,0:T(8,128)S(1)}, f32[8,8,16,128]{3,2,1,0:T(8,128)S(1)}, u32[]{:S(2)}, u32[]{:S(2)}) collective-permute-start(f32[8,8,16,128]{3,2,1,0:T(8,128)S(1)} %broadcast_select_fusion.5), channel_id=1, source_target_pairs={{0,1},{1,2},{2,3},{3,4},{4,5},{5,6},{6,7},{7,8},{8,9},{9,10},{10,1... | collective-permute-start | bytes 1572872 | tf_op jit(solution)/shard_map/ppermute | solution.py:191
  21.3 15.5 %collective-permute-start.2 = (f32[8,8,16,128]{3,2,1,0:T(8,128)S(1)}, f32[8,8,16,128]{3,2,1,0:T(8,128)S(1)}, u32[]{:S(2)}, u32[]{:S(2)}) collective-permute-start(f32[8,8,16,128]{3,2,1,0:T(8,128)S(1)} %broadcast_select_fusion), channel_id=1, source_target_pairs={{0,2},{1,3},{2,4},{3,5},{4,6},{5,7},{6,8},{7,9},{8,10},{9,11},{10,... | collective-permute-start | bytes 1572872 | tf_op jit(solution)/shard_map/ppermute | solution.py:191
  36.9 13.7 %collective-permute-start.3 = (f32[8,8,16,128]{3,2,1,0:T(8,128)S(1)}, f32[8,8,16,128]{3,2,1,0:T(8,128)S(1)}, u32[]{:S(2)}, u32[]{:S(2)}) collective-permute-start(f32[8,8,16,128]{3,2,1,0:T(8,128)S(1)} %broadcast_select_fusion.1), channel_id=1, source_target_pairs={{0,4},{1,5},{2,6},{3,7},{4,8},{5,9},{6,10},{7,11},{8,12},{9,13},{1... | collective-permute-start | bytes 1572872 | tf_op jit(solution)/shard_map/ppermute | solution.py:191
  50.8 36.5 %collective-permute-start.4 = (f32[8,8,16,128]{3,2,1,0:T(8,128)S(1)}, f32[8,8,16,128]{3,2,1,0:T(8,128)S(1)}, u32[]{:S(2)}, u32[]{:S(2)}) collective-permute-start(f32[8,8,16,128]{3,2,1,0:T(8,128)S(1)} %broadcast_select_fusion.2), channel_id=1, source_target_pairs={{0,8},{1,9},{2,10},{3,11},{4,12},{5,13},{6,14},{7,15},{8,16},{9,17... | collective-permute-start | bytes 1572872 | tf_op jit(solution)/shard_map/ppermute | solution.py:191
  87.4 25.3 %collective-permute-start.5 = (f32[8,8,16,128]{3,2,1,0:T(8,128)S(1)}, f32[8,8,16,128]{3,2,1,0:T(8,128)S(1)}, u32[]{:S(2)}, u32[]{:S(2)}) collective-permute-start(f32[8,8,16,128]{3,2,1,0:T(8,128)S(1)} %broadcast_select_fusion.3), channel_id=1, source_target_pairs={{0,16},{1,17},{2,18},{3,19},{4,20},{5,21},{6,22},{7,23},{8,24},{9,... | collective-permute-start | bytes 1572872 | tf_op jit(solution)/shard_map/ppermute | solution.py:191
  112.9 6.9 %collective-permute-start.6 = (f32[8,8,2,128]{3,2,1,0:T(2,128)S(1)}, f32[8,8,2,128]{3,2,1,0:T(2,128)S(1)}, u32[]{:S(2)}, u32[]{:S(2)}) collective-permute-start(f32[8,8,2,128]{3,2,1,0:T(2,128)S(1)} %get-tuple-element.13), channel_id=1, source_target_pairs={{0,32},{32,64},{64,96},{96,128},{128,160},{160,192},{192,224},{1,3... | collective-permute-start | bytes 196616 | tf_op jit(solution)/shard_map/ppermute | solution.py:201
  114.9 8.2 %collective-permute-start.7 = (f32[8,8,2,128]{3,2,1,0:T(2,128)S(1)}, f32[8,8,2,128]{3,2,1,0:T(2,128)S(1)}, u32[]{:S(2)}, u32[]{:S(2)}) collective-permute-start(f32[8,8,2,128]{3,2,1,0:T(2,128)S(1)} %get-tuple-element.14), channel_id=1, source_target_pairs={{32,0},{64,32},{96,64},{128,96},{160,128},{192,160},{224,192},{33,... | collective-permute-start | bytes 196616 | tf_op jit(solution)/shard_map/ppermute | solution.py:204
  123.8 19.0 %collective-permute-start.8 = (f32[64,128]{1,0:T(8,128)S(1)}, f32[64,128]{1,0:T(8,128)S(1)}, u32[]{:S(2)}, u32[]{:S(2)}) collective-permute-start(f32[64,128]{1,0:T(8,128)S(1)} %pad.7), channel_id=1, source_target_pairs={{0,1},{1,2},{2,3},{3,4},{4,5},{5,6},{6,7},{7,8},{8,9},{9,10},{10,1... | collective-permute-start | bytes 98312 | tf_op jit(solution)/shard_map/ppermute | solution.py:191
  141.6 3.4 %collective-permute-start.9 = (f32[64,128]{1,0:T(8,128)S(1)}, f32[64,128]{1,0:T(8,128)S(1)}, u32[]{:S(2)}, u32[]{:S(2)}) collective-permute-start(f32[64,128]{1,0:T(8,128)S(1)} %pad.8), channel_id=1, source_target_pairs={{0,31},{1,0},{2,1},{3,2},{4,3},{5,4},{6,5},{7,6},{8,7},{9,8},{10,9... | collective-permute-start | bytes 98312 | tf_op jit(solution)/shard_map/ppermute | solution.py:191
  142.7 2.3 %copy-start.1 = (f32[64,128]{1,0:T(8,128)}, f32[64,128]{1,0:T(8,128)S(1)}, u32[]{:S(2)}) copy-start(f32[64,128]{1,0:T(8,128)S(1)} %collective-permute-done.8.low_ref) | copy-start | bytes 98308
  145.0 0.6 copy-start.2

commit v2 on v1

--- a/solution.py
+++ b/solution.py
@@ -184,86 +184,281 @@
     )(rows_form, low, high)
     return out.reshape(8, 8, rows, width)
 
-
-def passed_along(value, axis, steps):
-    count = lax.axis_size(axis)
-    pairs = [(source, (source + steps) % count) for source in range(count)]
-    return lax.ppermute(value, axis, pairs)
-
-
-def with_halo(block, sides, width, periodic):
-    for axis, dim in sides:
-        count = lax.axis_size(axis)
-        forward = [(i, i + 1) for i in range(count - 1)]
-        if periodic:
-            forward.append((count - 1, 0))
-        backward = [(target, source) for source, target in forward]
-        low = lax.ppermute(
-            lax.slice_in_dim(block, block.shape[dim] - width, None, axis=dim), axis, forward
+MESH = pl.DeviceIdType.MESH
+HOPS = 5
+AHEAD, BACK = 5, 7
+SLOTS = AHEAD + BACK
+PARTS = 4
+
+
+def plan_kernel(rows, rings, shift_ref, plan_ref):
+    shape = (rows, 128)
+    low = lax.axis_index("az") % 4
+    down = lax.broadcasted_iota(jnp.int32, shape, 0)
+    along = lax.broadcasted_iota(jnp.int32, shape, 1)
+    amount = jnp.zeros(shape, jnp.int32)
+    other = jnp.full(shape, -1, jnp.int32)
+    for r in range(rows):
+        amount = jnp.where(down == r, shift_ref[r], amount)
+        other = jnp.where(along == r, shift_ref[r], other)
+    coarse, other_coarse = amount // 128, other // 128
+    chips = (low + coarse) // 4 % rings
+    other_chips = (low + other_coarse) // 4 % rings
+    real = along < rows
+    key, other_key = chips * rows + down, other_chips * rows + along
+    as_float = lambda x: x.astype(jnp.float32)
+    before = as_float(jnp.where(real & (other_key < key), 1, 0))
+    rank = jnp.sum(before, axis=1, keepdims=True)
+    after = as_float(jnp.where(key < other_key, 1, 0))
+    other_rank = jnp.sum(after, axis=0, keepdims=True)
+    chips_f, other_chips_f = as_float(chips), as_float(other_chips)
+    count = as_float(along)
+    ahead = rank < count
+    back_f = float(rings) - chips_f
+    load_ahead = jnp.sum(jnp.where(ahead, chips_f, 0.0), axis=0, keepdims=True)
+    load_back = jnp.sum(jnp.where(ahead, 0.0, back_f), axis=0, keepdims=True)
+    far_ahead = jnp.max(jnp.where(ahead, chips_f, 0.0), axis=0, keepdims=True)
+    far_back = jnp.max(jnp.where(ahead, 0.0, back_f), axis=0, keepdims=True)
+    fits = (load_ahead <= AHEAD * HOPS) & (load_back <= BACK * HOPS) & (far_ahead <= HOPS) & (far_back <= HOPS)
+    lanes_f = as_float(lax.broadcasted_iota(jnp.int32, (1, 128), 1))
+    cut = jnp.min(jnp.where(fits & (lanes_f <= float(rows)), lanes_f, 128.0), axis=1, keepdims=True)
+    back, other_back = rank >= cut, other_rank >= cut
+    hops = jnp.where(back, back_f, chips_f)
+    other_hops = jnp.where(other_back, float(rings) - other_chips_f, other_chips_f)
+    side_f = jnp.where(back, 1.0, 0.0)
+    other_side = jnp.where(other_back, 1.0, 0.0)
+    first = jnp.sum(before * other_hops * jnp.where(side_f == other_side, 1.0, 0.0), axis=1, keepdims=True)
+    hop = as_float(along)
+    reach = first - hop + float(HOPS - 1)
+    place = jnp.zeros(shape, jnp.float32)
+    for k in range(1, max(AHEAD, BACK) + 1):
+        place = place + jnp.where(reach >= float(HOPS * k), 1.0, 0.0)
+    there = place * float(HOPS) + hop < first + hops
+    arrival = jnp.where(there, place + side_f * float(AHEAD), -1.0)
+    within = amount - coarse * 128
+    turn = coarse % 4
+    crosses = (low % 2 + turn) // 2 % 2
+    table = jnp.where(along < HOPS, arrival.astype(jnp.int32), within)
+    table = jnp.where(along == HOPS + 1, crosses, table)
+    table = jnp.where(along == HOPS + 2, turn % 2, table)
+    plan_ref[0:rows, :] = table
+    slot = along % SLOTS
+    slot_back = jnp.where(slot >= AHEAD, 1.0, 0.0)
+    line = as_float(slot) - slot_back * float(AHEAD)
+    line = line * float(HOPS) + as_float(along // SLOTS)
+    inside = (side_f == slot_back) & (first <= line) & (line < first + hops)
+    chosen = jnp.sum(jnp.where(inside, as_float(down), 0.0), axis=0, keepdims=True)
+    plan_ref[rows:rows + 8, :] = jnp.broadcast_to(chosen, (8, 128)).astype(jnp.int32)
+
+
+def travel_kernel(
+    rows, n_az, n_rad, state_ref, plan_ref, out_ref, low_ref, high_ref,
+    before_ref, cur_ref, pack_ref, come_ref, across_ref, twin_ref, under_ref, over_ref, edge_ref, edge_in_ref,
+    send_sem, recv_sem,
+):
+    az, rad = lax.axis_index("az"), lax.axis_index("rad")
+    low_bits = az % 4
+    step_az = lambda k: {"az": (az + k + n_az) % n_az}
+    next_az, prev_az, next_z, prev_z = step_az(1), step_az(-1), step_az(4), step_az(-4)
+    across = {"az": az + 2 - 4 * (low_bits // 2)}
+    twin = {"az": az + 1 - 2 * (az % 2)}
+    above = {"rad": (rad + 1) % n_rad}
+    below = {"rad": (rad + n_rad - 1) % n_rad}
+    barrier = pltpu.get_barrier_semaphore()
+    partners = [next_az, prev_az, next_z, prev_z, across, twin, above, below]
+    for device in partners:
+        pl.semaphore_signal(barrier, inc=1, device_id=device, device_id_type=MESH)
+    pl.semaphore_wait(barrier, len(partners))
+
+    fields = 8 // PARTS
+    deep = fields * 8
+    lane = lax.broadcasted_iota(jnp.int32, (8, 128), 1)
+    count = [0]
+    copies = {}
+
+    def send(name, src, dst, device):
+        copy = pltpu.make_async_remote_copy(
+            src_ref=src, dst_ref=dst, send_sem=send_sem.at[count[0]], recv_sem=recv_sem.at[count[0]],
+            device_id=device, device_id_type=MESH,
         )
-        high = lax.ppermute(lax.slice_in_dim(block, 0, width, axis=dim), axis, backward)
-        block = jnp.concatenate([low, block, high], axis=dim)
-    return block
-
-
-def outflow(padded, place, last_place):
-    inner = padded[:, :, 2:-2]
-    lower = jnp.where(
-        place == 0, jnp.broadcast_to(inner[:, :, :1], padded[:, :, :2].shape), padded[:, :, :2]
-    )
-    upper = jnp.where(
-        place == last_place,
-        jnp.broadcast_to(inner[:, :, -1:], padded[:, :, -2:].shape),
-        padded[:, :, -2:],
-    )
-    return jnp.concatenate([lower, inner, upper], axis=2)
-
-
-def rotate_local(values, amount):
-    row_width = values.shape[-1]
-    last_axis = values.ndim - 1
-    for bit_level in range((row_width - 1).bit_length()):
-        rolled = jnp.roll(values, 1 << bit_level, axis=last_axis)
-        chosen = amount // (1 << bit_level) % 2 == 1
-        values = jnp.where(chosen[:, None], rolled, values)
-    return values
-
-
-def per_device(state, shift):
-    row_count = state.shape[2]
-    col_count = state.shape[3]
-    column = lax.broadcasted_iota(jnp.int32, (row_count, col_count), 1)
-    residual = shift % col_count
-    coarse = shift // col_count
-    rolled = rotate_local(state, residual)
-    carried = passed_along(rolled, "az", 1)
-    remapped = jnp.where((column >= residual[:, None])[None, None], rolled, carried)
-    for bit_level in range((lax.axis_size("az") - 1).bit_length()):
-        arrived = passed_along(remapped, "az", 1 << bit_level)
-        chosen = coarse // (1 << bit_level) % 2 == 1
-        remapped = jnp.where(chosen[None, None, :, None], arrived, remapped)
-    place = lax.axis_index("rad")
-    last_place = lax.axis_size("rad") - 1
-    radial = with_halo(remapped, (("rad", 2),), 2, False)
-    radial = outflow(radial, place, last_place)[:, :, 1:]
-    rows_form = radial.transpose(2, 0, 1, 3).reshape(row_count + 3, 64, col_count)
-
-    def edge(cells, steps):
-        flat = cells.reshape(64, 2 * (row_count + 3))
-        flat = jnp.pad(flat, ((0, 0), (0, col_count - flat.shape[1])))
-        return passed_along(flat, "az", steps)
-
-    low = edge(radial[..., -2:], 1)
-    high = edge(radial[..., :2], -1)
-    return step(rows_form, low, high)
+        count[0] += 1
+        copies[name] = copy
+        copy.start()
+
+    def each(n, width, fn):
+        def some(i, _):
+            for j in range(width):
+                fn(i * width + j)
+            return 0
+        lax.fori_loop(0, n // width, some, 0)
+
+    def depart(c, hop):
+        def one(m):
+            r = plan_ref[rows, hop * SLOTS + m]
+            pack_ref[hop, c, m] = cur_ref[hop, c, r]
+        each(SLOTS, 4, one)
+        send(("ahead", c, hop), pack_ref.at[hop, c, 0:AHEAD], come_ref[hop * PARTS + c].at[0:AHEAD], next_z)
+        send(("back", c, hop), pack_ref.at[hop, c, AHEAD:SLOTS], come_ref[hop * PARTS + c].at[AHEAD:SLOTS], prev_z)
+
+    def merge(c, level, flag_lane, source):
+        def one(r):
+            flag = jnp.full((deep, 128), plan_ref[r, flag_lane], jnp.int32)
+            cur_ref[level + 1, c, r] = jnp.where(flag == 1, source[c, r], cur_ref[level, c, r])
+        each(rows, 4, one)
+
+    def stage(k, c):
+        if k == 0:
+            part = pl.ds(c * fields * 8 * rows, fields * 8 * rows)
+            send(("carry", c), state_ref.at[part], before_ref.at[part], next_az)
+        elif k == 1:
+            copies["carry", c].wait_recv()
+
+            def one(r):
+                amount = plan_ref[r, HOPS]
+                bound = jnp.full((8, 128), 128 - amount, jnp.int32)
+                for f in range(fields):
+                    cells = pl.ds((c * fields + f) * 8 * rows + r, 8, stride=rows)
+                    mixed = jnp.where(lane < bound, state_ref[cells, :], before_ref[cells, :])
+                    cur_ref[0, c, r, f * 8:(f + 1) * 8, :] = pltpu.roll(mixed, amount, 1)
+            each(rows, 4, one)
+            depart(c, 0)
+        elif k <= 1 + HOPS:
+            hop = k - 2
+            copies["ahead", c, hop].wait_recv()
+            copies["back", c, hop].wait_recv()
+
+            def one(r):
+                slot = plan_ref[r, hop]
+                come = come_ref[hop * PARTS + c][jnp.maximum(slot, 0)]
+                flag = jnp.full((deep, 128), slot, jnp.int32)
+                cur_ref[hop + 1, c, r] = jnp.where(flag >= 0, come, cur_ref[hop, c, r])
+            each(rows, 4, one)
+            if hop + 1 < HOPS:
+                depart(c, hop + 1)
+            else:
+                send(("across", c), cur_ref.at[HOPS, c], across_ref.at[c], across)
+        elif k == 2 + HOPS:
+            copies["across", c].wait_recv()
+            merge(c, HOPS, HOPS + 1, across_ref)
+            send(("twin", c), cur_ref.at[HOPS + 1, c], twin_ref.at[c], twin)
+        elif k == 3 + HOPS:
+            copies["twin", c].wait_recv()
+            merge(c, HOPS + 1, HOPS + 2, twin_ref)
+            tall = 2 if c * fields <= 4 < (c + 1) * fields else 1
+            final = cur_ref.at[HOPS + 2, c]
+            send(("up", c), final.at[rows - 1:rows], under_ref.at[c], above)
+            send(("down", c), final.at[0:tall], over_ref.at[c, 0:tall], below)
+
+            def one(r):
+                out_ref[r + 1, c * deep:(c + 1) * deep, :] = cur_ref[HOPS + 2, c, r]
+            each(rows, 4, one)
+
+    stages = 4 + HOPS
+    for wave in range(stages + PARTS - 1):
+        for c in range(PARTS):
+            if 0 <= wave - c < stages:
+                stage(wave - c, c)
+
+    last = HOPS + 2
+
+    def edges(f, get, first, n, low, high):
+        for q in range(first, first + n):
+            x = get(q)
+            low = jnp.where(lane // 2 == q, pltpu.roll(x, (2 * q + 2) % 128, 1), low)
+            high = jnp.where(lane // 2 == q, pltpu.roll(x, 2 * q, 1), high)
+        return low, high
+
+    for f in range(8):
+        c, at = f // fields, (f % fields) * 8
+        low = high = jnp.ones((8, 128), jnp.float32)
+        low, high = edges(f, lambda q: cur_ref[last, c, q - 1, at:at + 8, :], 1, rows, low, high)
+        edge_ref[0, f * 8:(f + 1) * 8, :] = low
+        edge_ref[1, f * 8:(f + 1) * 8, :] = high
+    at_start = jnp.full((8, 128), rad, jnp.int32) == 0
+    at_end = jnp.full((8, 128), rad, jnp.int32) == n_rad - 1
+    for c in range(PARTS):
+        copies["up", c].wait_recv()
+        copies["down", c].wait_recv()
+        for f in range(fields):
+            here = slice((c * fields + f) * 8, (c * fields + f + 1) * 8)
+            at = slice(f * 8, f * 8 + 8)
+            top = cur_ref[last, c, rows - 1, at, :]
+            under = jnp.where(at_start, cur_ref[last, c, 0, at, :], under_ref[c, 0, at, :])
+            over = jnp.where(at_end, top, over_ref[c, 0, at, :])
+            beyond = top
+            if c * fields + f == 4:
+                beyond = jnp.where(at_end, top, over_ref[c, 1, at, :])
+            out_ref[0, here, :] = under
+            out_ref[rows + 1, here, :] = over
+            out_ref[rows + 2, here, :] = beyond
+            halo = {0: under, rows + 1: over, rows + 2: beyond}
+            low, high = edge_ref[0, here, :], edge_ref[1, here, :]
+            low, high = edges(f, lambda q: halo[q], 0, 1, low, high)
+            low, high = edges(f, lambda q: halo[q], rows + 1, 2, low, high)
+            edge_ref[2, here, :] = low
+            edge_ref[3, here, :] = high
+    send("low", edge_ref.at[2], edge_in_ref.at[0], next_az)
+    send("high", edge_ref.at[3], edge_in_ref.at[1], prev_az)
+    copies["low"].wait_recv()
+    low_ref[...] = edge_in_ref[0]
+    copies["high"].wait_recv()
+    high_ref[...] = edge_in_ref[1]
+    for copy in copies.values():
+        copy.wait_send()
+
+
+def travel(state, shift, n_az, n_rad):
+    rows, width = state.shape[2], state.shape[3]
+    plan = pl.pallas_call(
+        functools.partial(plan_kernel, rows, n_az // 4),
+        out_shape=jax.ShapeDtypeStruct((rows + 8, 128), jnp.int32),
+        in_specs=[pl.BlockSpec(memory_space=pltpu.SMEM)],
+        out_specs=pl.BlockSpec(memory_space=pltpu.VMEM),
+        name="plan_routes",
+    )(shift)
+    deep = 64 // PARTS
+    f32 = jnp.float32
+    vmem = pl.BlockSpec(memory_space=pltpu.VMEM)
+    n_copies = PARTS * (5 + 2 * HOPS) + 2
+    return pl.pallas_call(
+        functools.partial(travel_kernel, rows, n_az, n_rad),
+        out_shape=[
+            jax.ShapeDtypeStruct((rows + 3, 64, width), f32),
+            jax.ShapeDtypeStruct((64, width), f32),
+            jax.ShapeDtypeStruct((64, width), f32),
+        ],
+        in_specs=[vmem, pl.BlockSpec(memory_space=pltpu.SMEM)],
+        out_specs=[vmem] * 3,
+        scratch_shapes=[
+            pltpu.VMEM((64 * rows, width), f32),
+            pltpu.VMEM((HOPS + 3, PARTS, rows, deep, width), f32),
+            pltpu.VMEM((HOPS, PARTS, SLOTS, deep, width), f32),
+            [pltpu.VMEM((SLOTS, deep, width), f32)] * (HOPS * PARTS),
+            pltpu.VMEM((PARTS, rows, deep, width), f32),
+            pltpu.VMEM((PARTS, rows, deep, width), f32),
+            pltpu.VMEM((PARTS, 1, deep, width), f32),
+            pltpu.VMEM((PARTS, 2, deep, width), f32),
+            pltpu.VMEM((4, 64, width), f32),
+            pltpu.VMEM((2, 64, width), f32),
+            pltpu.SemaphoreType.DMA((n_copies,)),
+            pltpu.SemaphoreType.DMA((n_copies,)),
+        ],
+        compiler_params=pltpu.CompilerParams(collective_id=0, has_side_effects=True),
+        name="travel_rows",
+    )(state.reshape(64 * rows, width), plan)
 
 
 def solution(mesh):
-    placed = (P(None, None, "rad", "az"), P("rad"))
+    n_az, n_rad = mesh.shape["az"], mesh.shape["rad"]
+
+    def per_device(state, shift):
+        rows_form, low, high = travel(state, shift, n_az, n_rad)
+        return step(rows_form, low, high)
+
     return jax.shard_map(
         per_device,
         mesh=mesh,
-        in_specs=placed,
+        in_specs=(P(None, None, "rad", "az"), P("rad")),
         out_specs=P(None, None, "rad", "az"),
         check_vma=False,
     )

time: 155 us -> 74.2 us (0.48)
  the two profiles are of different devices: /device:TPU:109 before, /device:TPU:1 now
where the time goes in v2:
time: 74.2 us; the launch traced here: 73.6 us
  Pallas kernels  73.6 us (99%)
    pallas_call x1, Pallas kernels, travel(): pl.pallas_call(functools.partial(travel_kernel, rows, n_az, n_rad), out_s...  62.9 us
    pallas_call x1, Pallas kernels, step(): pl.pallas_call(functools.partial(step_kernel, rows), out_shape=jax.ShapeD...  9.17 us
    pallas_call x1, Pallas kernels, travel(): pl.pallas_call(functools.partial(plan_kernel, rows, n_az // 4), out_shape...  1.56 us

profile of v2, /device:TPU:1, one launch (start us, length us, event | category | flops | bytes accessed | tf_op | source)
XLA Modules:
  0.0 73.6 jit_solution(4507032190370079868)
XLA Ops:
  0.0 1.6 %plan_routes.1.plan_ref = s32[24,128]{1,0:T(8,128)} custom-call(s32[16]{0:T(128)} %shift_ref.1), custom_call_target="tpu_custom_call" | custom-call | tf_op jit(solution)/shard_map/plan_routes/pallas_call | solution.py:412
  1.6 62.9 %travel_rows.1 = (f32[19,64,128]{2,1,0:T(8,128)}, f32[64,128]{1,0:T(8,128)}, f32[64,128]{1,0:T(8,128)}) custom-call(f32[1024,128]{1,0:T(8,128)} %bitcast.2, s32[24,128]{1,0:T(8,128)} %plan_routes.1.plan_ref), custom_call_target="tpu_custom_call" | custom-call | tf_op jit(solution)/shard_map/travel_rows/pallas_call | solution.py:423
  64.5 9.2 %advance_rows.1 = f32[1024,128]{1,0:T(8,128)} custom-call(f32[19,64,128]{2,1,0:T(8,128)} %get-tuple-element.8.rows_ref, f32[64,128]{1,0:T(8,128)} %get-tuple-element.9.low_ref, f32[64,128]{1,0:T(8,128)} %get-tuple-element.10.high_ref), custom_call_target="tpu_custom_call" | custom-call | tf_op jit(solution)/shard_map/advance_rows/pallas_call | solution.py:177

commit v3 on v2

--- a/solution.py
+++ b/solution.py
@@ -352,57 +352,63 @@
             def one(r):
                 out_ref[r + 1, c * deep:(c + 1) * deep, :] = cur_ref[HOPS + 2, c, r]
             each(rows, 4, one)
-
-    stages = 4 + HOPS
-    for wave in range(stages + PARTS - 1):
-        for c in range(PARTS):
-            if 0 <= wave - c < stages:
-                stage(wave - c, c)
+            for f in range(fields):
+                here = slice((c * fields + f) * 8, (c * fields + f + 1) * 8)
+                at = slice(f * 8, f * 8 + 8)
+                low = high = jnp.ones((8, 128), jnp.float32)
+                low, high = edges(lambda q: cur_ref[last, c, q - 1, at, :], 1, rows, low, high)
+                edge_ref[0, here, :] = low
+                edge_ref[1, here, :] = high
+        elif k == 4 + HOPS:
+            copies["up", c].wait_recv()
+            copies["down", c].wait_recv()
+            for f in range(fields):
+                here = slice((c * fields + f) * 8, (c * fields + f + 1) * 8)
+                at = slice(f * 8, f * 8 + 8)
+                top = cur_ref[last, c, rows - 1, at, :]
+                under = jnp.where(at_start, cur_ref[last, c, 0, at, :], under_ref[c, 0, at, :])
+                over = jnp.where(at_end, top, over_ref[c, 0, at, :])
+                beyond = top
+                if c * fields + f == 4:
+                    beyond = jnp.where(at_end, top, over_ref[c, 1, at, :])
+                out_ref[0, here, :] = under
+                out_ref[rows + 1, here, :] = over
+                out_ref[rows + 2, here, :] = beyond
+                halo = {0: under, rows + 1: over, rows + 2: beyond}
+                low, high = edge_ref[0, here, :], edge_ref[1, here, :]
+                low, high = edges(lambda q: halo[q], 0, 1, low, high)
+                low, high = edges(lambda q: halo[q], rows + 1, 2, low, high)
+                edge_ref[2, here, :] = low
+                edge_ref[3, here, :] = high
+            part = slice(c * deep, (c + 1) * deep)
+            send(("low", c), edge_ref.at[2, part], edge_in_ref.at[0, part], next_az)
+            send(("high", c), edge_ref.at[3, part], edge_in_ref.at[1, part], prev_az)
+        elif k == 5 + HOPS:
+            part = slice(c * deep, (c + 1) * deep)
+            copies["low", c].wait_recv()
+            low_ref[part, :] = edge_in_ref[0, part, :]
+            copies["high", c].wait_recv()
+            high_ref[part, :] = edge_in_ref[1, part, :]
 
     last = HOPS + 2
-
-    def edges(f, get, first, n, low, high):
+    at_start = jnp.full((8, 128), rad, jnp.int32) == 0
+    at_end = jnp.full((8, 128), rad, jnp.int32) == n_rad - 1
+
+    def edges(get, first, n, low, high):
         for q in range(first, first + n):
             x = get(q)
             low = jnp.where(lane // 2 == q, pltpu.roll(x, (2 * q + 2) % 128, 1), low)
             high = jnp.where(lane // 2 == q, pltpu.roll(x, 2 * q, 1), high)
         return low, high
 
-    for f in range(8):
-        c, at = f // fields, (f % fields) * 8
-        low = high = jnp.ones((8, 128), jnp.float32)
-        low, high = edges(f, lambda q: cur_ref[last, c, q - 1, at:at + 8, :], 1, rows, low, high)
-        edge_ref[0, f * 8:(f + 1) * 8, :] = low
-        edge_ref[1, f * 8:(f + 1) * 8, :] = high
-    at_start = jnp.full((8, 128), rad, jnp.int32) == 0
-    at_end = jnp.full((8, 128), rad, jnp.int32) == n_rad - 1
     for c in range(PARTS):
-        copies["up", c].wait_recv()
-        copies["down", c].wait_recv()
-        for f in range(fields):
-            here = slice((c * fields + f) * 8, (c * fields + f + 1) * 8)
-            at = slice(f * 8, f * 8 + 8)
-            top = cur_ref[last, c, rows - 1, at, :]
-            under = jnp.where(at_start, cur_ref[last, c, 0, at, :], under_ref[c, 0, at, :])
-            over = jnp.where(at_end, top, over_ref[c, 0, at, :])
-            beyond = top
-            if c * fields + f == 4:
-                beyond = jnp.where(at_end, top, over_ref[c, 1, at, :])
-            out_ref[0, here, :] = under
-            out_ref[rows + 1, here, :] = over
-            out_ref[rows + 2, here, :] = beyond
-            halo = {0: under, rows + 1: over, rows + 2: beyond}
-            low, high = edge_ref[0, here, :], edge_ref[1, here, :]
-            low, high = edges(f, lambda q: halo[q], 0, 1, low, high)
-            low, high = edges(f, lambda q: halo[q], rows + 1, 2, low, high)
-            edge_ref[2, here, :] = low
-            edge_ref[3, here, :] = high
-    send("low", edge_ref.at[2], edge_in_ref.at[0], next_az)
-    send("high", edge_ref.at[3], edge_in_ref.at[1], prev_az)
-    copies["low"].wait_recv()
-    low_ref[...] = edge_in_ref[0]
-    copies["high"].wait_recv()
-    high_ref[...] = edge_in_ref[1]
+        stage(0, c)
+    stages = 6 + HOPS
+    for wave in range(1, stages + PARTS - 1):
+        for c in range(PARTS):
+            if 1 <= wave - c < stages:
+                stage(wave - c, c)
+
     for copy in copies.values():
         copy.wait_send()
 
@@ -419,7 +425,7 @@
     deep = 64 // PARTS
     f32 = jnp.float32
     vmem = pl.BlockSpec(memory_space=pltpu.VMEM)
-    n_copies = PARTS * (5 + 2 * HOPS) + 2
+    n_copies = PARTS * (7 + 2 * HOPS)
     return pl.pallas_call(
         functools.partial(travel_kernel, rows, n_az, n_rad),
         out_shape=[

time: 74.2 us -> 78.8 us (1.062)
  Pallas kernels: 73.6 us -> 78.7 us
    pallas_call x1, Pallas kernels: 62.9 us -> 68 us  [travel(): pl.pallas_call(functools.partial(travel_kernel, rows, n_az, n_rad), out_s...]
where the time goes in v3:
time: 78.8 us; the launch traced here: 78.7 us
  Pallas kernels  78.7 us (100%)
    pallas_call x1, Pallas kernels, travel(): pl.pallas_call(functools.partial(travel_kernel, rows, n_az, n_rad), out_s...  68 us
    pallas_call x1, Pallas kernels, step(): pl.pallas_call(functools.partial(step_kernel, rows), out_shape=jax.ShapeD...  9.17 us

profile of v3, /device:TPU:1, one launch (start us, length us, event | category | flops | bytes accessed | tf_op | source)
XLA Modules:
  0.0 78.7 jit_solution(2772189865066093883)
XLA Ops:
  0.0 1.6 %plan_routes.1.plan_ref = s32[24,128]{1,0:T(8,128)} custom-call(s32[16]{0:T(128)} %shift_ref.1), custom_call_target="tpu_custom_call" | custom-call | tf_op jit(solution)/shard_map/plan_routes/pallas_call | solution.py:418
  1.6 68.0 %travel_rows.1 = (f32[19,64,128]{2,1,0:T(8,128)}, f32[64,128]{1,0:T(8,128)}, f32[64,128]{1,0:T(8,128)}) custom-call(f32[1024,128]{1,0:T(8,128)} %bitcast.2, s32[24,128]{1,0:T(8,128)} %plan_routes.1.plan_ref), custom_call_target="tpu_custom_call" | custom-call | tf_op jit(solution)/shard_map/travel_rows/pallas_call | solution.py:429
  69.5 9.2 %advance_rows.1 = f32[1024,128]{1,0:T(8,128)} custom-call(f32[19,64,128]{2,1,0:T(8,128)} %get-tuple-element.8.rows_ref, f32[64,128]{1,0:T(8,128)} %get-tuple-element.9.low_ref, f32[64,128]{1,0:T(8,128)} %get-tuple-element.10.high_ref), custom_call_target="tpu_custom_call" | custom-call | tf_op jit(solution)/shard_map/advance_rows/pallas_call | solution.py:177

commit v4 on v2

--- a/solution.py
+++ b/solution.py
@@ -285,26 +285,26 @@
         copies[name] = copy
         copy.start()
 
-    def each(n, width, fn):
-        def some(i, _):
-            for j in range(width):
-                fn(i * width + j)
-            return 0
-        lax.fori_loop(0, n // width, some, 0)
+    def each(n, load, store):
+        values = [load(i) for i in range(n)]
+        for i in range(n):
+            store(i, values[i])
 
     def depart(c, hop):
-        def one(m):
-            r = plan_ref[rows, hop * SLOTS + m]
-            pack_ref[hop, c, m] = cur_ref[hop, c, r]
-        each(SLOTS, 4, one)
+        def put(m, x):
+            pack_ref[hop, c, m] = x
+        each(SLOTS, lambda m: cur_ref[hop, c, plan_ref[rows, hop * SLOTS + m]], put)
         send(("ahead", c, hop), pack_ref.at[hop, c, 0:AHEAD], come_ref[hop * PARTS + c].at[0:AHEAD], next_z)
         send(("back", c, hop), pack_ref.at[hop, c, AHEAD:SLOTS], come_ref[hop * PARTS + c].at[AHEAD:SLOTS], prev_z)
 
     def merge(c, level, flag_lane, source):
         def one(r):
             flag = jnp.full((deep, 128), plan_ref[r, flag_lane], jnp.int32)
-            cur_ref[level + 1, c, r] = jnp.where(flag == 1, source[c, r], cur_ref[level, c, r])
-        each(rows, 4, one)
+            return jnp.where(flag == 1, source[c, r], cur_ref[level, c, r])
+
+        def put(r, x):
+            cur_ref[level + 1, c, r] = x
+        each(rows, one, put)
 
     def stage(k, c):
         if k == 0:
@@ -316,11 +316,17 @@
             def one(r):
                 amount = plan_ref[r, HOPS]
                 bound = jnp.full((8, 128), 128 - amount, jnp.int32)
+                found = []
                 for f in range(fields):
                     cells = pl.ds((c * fields + f) * 8 * rows + r, 8, stride=rows)
                     mixed = jnp.where(lane < bound, state_ref[cells, :], before_ref[cells, :])
-                    cur_ref[0, c, r, f * 8:(f + 1) * 8, :] = pltpu.roll(mixed, amount, 1)
-            each(rows, 4, one)
+                    found.append(pltpu.roll(mixed, amount, 1))
+                return found
+
+            def put(r, found):
+                for f in range(fields):
+                    cur_ref[0, c, r, f * 8:(f + 1) * 8, :] = found[f]
+            each(rows, one, put)
             depart(c, 0)
         elif k <= 1 + HOPS:
             hop = k - 2
@@ -331,8 +337,11 @@
                 slot = plan_ref[r, hop]
                 come = come_ref[hop * PARTS + c][jnp.maximum(slot, 0)]
                 flag = jnp.full((deep, 128), slot, jnp.int32)
-                cur_ref[hop + 1, c, r] = jnp.where(flag >= 0, come, cur_ref[hop, c, r])
-            each(rows, 4, one)
+                return jnp.where(flag >= 0, come, cur_ref[hop, c, r])
+
+            def put(r, x):
+                cur_ref[hop + 1, c, r] = x
+            each(rows, one, put)
             if hop + 1 < HOPS:
                 depart(c, hop + 1)
             else:
@@ -349,9 +358,9 @@
             send(("up", c), final.at[rows - 1:rows], under_ref.at[c], above)
             send(("down", c), final.at[0:tall], over_ref.at[c, 0:tall], below)
 
-            def one(r):
-                out_ref[r + 1, c * deep:(c + 1) * deep, :] = cur_ref[HOPS + 2, c, r]
-            each(rows, 4, one)
+            def put(r, x):
+                out_ref[r + 1, c * deep:(c + 1) * deep, :] = x
+            each(rows, lambda r: cur_ref[HOPS + 2, c, r], put)
 
     stages = 4 + HOPS
     for wave in range(stages + PARTS - 1):

time: 74.2 us -> 73.6 us (level)
  no operation moved by 1% of the time
where the time goes in v4:
time: 73.6 us; the launch traced here: 73 us
  Pallas kernels  72.9 us (99%)
    pallas_call x1, Pallas kernels, travel(): pl.pallas_call(functools.partial(travel_kernel, rows, n_az, n_rad), out_s...  62.2 us
    pallas_call x1, Pallas kernels, step(): pl.pallas_call(functools.partial(step_kernel, rows), out_shape=jax.ShapeD...  9.17 us
    pallas_call x1, Pallas kernels, travel(): pl.pallas_call(functools.partial(plan_kernel, rows, n_az // 4), out_shape...  1.56 us

profile of v4, /device:TPU:1, one launch (start us, length us, event | category | flops | bytes accessed | tf_op | source)
XLA Modules:
  0.0 73.0 jit_solution(14803623004427651769)
XLA Ops:
  0.0 1.6 %plan_routes.1.plan_ref = s32[24,128]{1,0:T(8,128)} custom-call(s32[16]{0:T(128)} %shift_ref.1), custom_call_target="tpu_custom_call" | custom-call | tf_op jit(solution)/shard_map/plan_routes/pallas_call | solution.py:421
  1.6 62.2 %travel_rows.1 = (f32[19,64,128]{2,1,0:T(8,128)}, f32[64,128]{1,0:T(8,128)}, f32[64,128]{1,0:T(8,128)}) custom-call(f32[1024,128]{1,0:T(8,128)} %bitcast.2, s32[24,128]{1,0:T(8,128)} %plan_routes.1.plan_ref), custom_call_target="tpu_custom_call" | custom-call | tf_op jit(solution)/shard_map/travel_rows/pallas_call | solution.py:432
  63.8 9.2 %advance_rows.1 = f32[1024,128]{1,0:T(8,128)} custom-call(f32[19,64,128]{2,1,0:T(8,128)} %get-tuple-element.8.rows_ref, f32[64,128]{1,0:T(8,128)} %get-tuple-element.9.low_ref, f32[64,128]{1,0:T(8,128)} %get-tuple-element.10.high_ref), custom_call_target="tpu_custom_call" | custom-call | tf_op jit(solution)/shard_map/advance_rows/pallas_call | solution.py:177
